TPU v7x, 32 devices: a whole 2x2x4 slice. The times are simulated.
32 devices in a mesh: batch: 8 (over z, y), tp: 4 (over x, core).
Axes of the slice: x: 2, y: 2, z: 4, core: 2. Of those that a mesh axis runs over, the one named last changes fastest.
Arguments:
- tokens: bfloat16 [2, 8192, 768], P(None, ('batch', 'tp')), may hold values from -6 to 6
- passage_lengths: int32 [2, 32], P(None, 'batch'), may hold values from 1 to 256, 5120 in all within a row
- cotangent: bfloat16 [2, 8192, 768], P(None, ('batch', 'tp')), may hold values from -6 to 6
- w_qkv: bfloat16 [768, 3, 768], P(None, None, 'tp'), may hold values from -0.21875 to 0.21875
- b_query: float32 [768], P('tp'), may hold values from -3 to 3
- b_value: float32 [768], P('tp'), may hold values from -3 to 3
- w_out: bfloat16 [768, 768], P('tp'), may hold values from -0.625 to 0.625
- b_out: float32 [768], replicated, may hold values from -2 to 2
- gain_one: float32 [768], replicated, may hold values from 0.5 to 1.5
- shift_one: float32 [768], replicated, may hold values from -2 to 2
- w_in: bfloat16 [768, 3072], P(None, 'tp'), may hold values from -0.21875 to 0.21875
- b_in: bfloat16 [3072], P('tp'), may hold values from -3 to 3
- w_back: bfloat16 [3072, 768], P('tp'), may hold values from -0.109375 to 0.109375
- b_back: float32 [768], replicated, may hold values from -2 to 2
- gain_two: float32 [768], replicated, may hold values from 0.5 to 1.5
- shift_two: float32 [768], replicated, may hold values from -2 to 2
Outputs:
- layer_out: bfloat16 [2, 8192, 768], P(None, ('batch', 'tp'))
- grad_tokens: float32 [2, 8192, 768], P(None, ('batch', 'tp'))
- grad_qkv: float32 [768, 3, 768], P(None, None, 'tp')
- grad_query_bias: float32 [768], P('tp')
- grad_value_bias: float32 [768], P('tp')
- grad_out: float32 [768, 768], P('tp')
- grad_out_bias: float32 [768], replicated
- grad_gain_one: float32 [768], replicated
- grad_shift_one: float32 [768], replicated
- grad_in: float32 [768, 3072], P(None, 'tp')
- grad_in_bias: float32 [3072], P('tp')
- grad_back: float32 [3072, 768], P('tp')
- grad_back_bias: float32 [768], replicated
- grad_gain_two: float32 [768], replicated
- grad_shift_two: float32 [768], replicated
Inputs may be any that keep to these rules, and one draw needn't show every extreme that they name: `passage_lengths`: each micro-batch's lengths, over all its passages together, sum to 5/8 of its 8192 slots, and some passage of every micro-batch fills all 256 slots.
All inputs are finite; a program needn't handle non-finite values. No bound on the sum of `passage_lengths` on one device may be relied on, other than what follows from the above.
Results may differ from a plain program's by a relative error of at most 0.013.
The roundings to bfloat16 on the way count: a program that leaves them out, or rounds other values in their place, can miss the bound.
Values may be sent and summed in bfloat16 or wider, within the bound.
No kernel may reach another device: no remote copies, remote signals or barrier semaphores. Data moves between devices by JAX's collectives and lax.ppermute only.
A program may use at most 128 MiB of HBM per device.

v0:
```python
import math

import jax
import jax.numpy as jnp
from jax import lax
from jax.sharding import PartitionSpec as P

DH = 64


epsilon = 1e-05


def norm_forward(values_in, gain_vec, shift_vec):
    middle = jnp.mean(values_in, axis=-1, keepdims=True)
    centred = values_in - middle
    spread = jnp.mean(centred * centred, axis=-1, keepdims=True)
    inverse = lax.rsqrt(spread + epsilon)
    unit_rows = centred * inverse
    return (unit_rows * gain_vec + shift_vec, unit_rows, inverse)


def norm_backward(grad_rows, unit_rows, inverse, gain_vec):
    scaled = grad_rows * gain_vec
    mean_one = jnp.mean(scaled, axis=-1, keepdims=True)
    mean_two = jnp.mean(scaled * unit_rows, axis=-1, keepdims=True)
    return inverse * (scaled - mean_one - unit_rows * mean_two)


def gelu_slope(preact):
    normal_cdf = 0.5 * (1.0 + lax.erf(preact * (1.0 / math.sqrt(2.0))))
    density = jnp.exp(-0.5 * preact * preact) * (1.0 / math.sqrt(2.0 * math.pi))
    return normal_cdf + preact * density


def attend_forward(qkv_blocks, key_keep, score_scale):
    queries = qkv_blocks[:, :, 0]
    key_rows = qkv_blocks[:, :, 1]
    value_rows = qkv_blocks[:, :, 2]
    scores = (
        jnp.einsum("pqhd,pkhd->phqk", queries, key_rows, preferred_element_type=jnp.float32)
        * score_scale
    )
    scores = jnp.where(key_keep[:, None, None, :], scores, -1000000000.0)
    row_max = jnp.max(scores, axis=-1, keepdims=True)
    exponent = jnp.exp(scores - row_max)
    row_total = jnp.sum(exponent, axis=-1, keepdims=True)
    attn_probs = exponent / row_total
    log_total = row_max + jnp.log(row_total)
    context = jnp.einsum(
        "phqk,pkhd->pqhd",
        attn_probs.astype(jnp.bfloat16),
        value_rows,
        preferred_element_type=jnp.float32,
    )
    return (context.astype(jnp.bfloat16), log_total)


def attend_backward(qkv_blocks, key_keep, log_total, grad_context, score_scale):
    queries = qkv_blocks[:, :, 0]
    key_rows = qkv_blocks[:, :, 1]
    value_rows = qkv_blocks[:, :, 2]
    scores = (
        jnp.einsum("pqhd,pkhd->phqk", queries, key_rows, preferred_element_type=jnp.float32)
        * score_scale
    )
    scores = jnp.where(key_keep[:, None, None, :], scores, -1000000000.0)
    attn_probs = jnp.exp(scores - log_total)
    grad_values = jnp.einsum(
        "phqk,pqhd->pkhd",
        attn_probs.astype(jnp.bfloat16),
        grad_context,
        preferred_element_type=jnp.float32,
    )
    grad_probs = jnp.einsum(
        "pqhd,pkhd->phqk", grad_context, value_rows, preferred_element_type=jnp.float32
    )
    row_delta = jnp.sum(attn_probs * grad_probs, axis=-1, keepdims=True)
    grad_scores = (attn_probs * (grad_probs - row_delta)).astype(jnp.bfloat16)
    grad_queries = (
        jnp.einsum("phqk,pkhd->pqhd", grad_scores, key_rows, preferred_element_type=jnp.float32)
        * score_scale
    )
    grad_keys = (
        jnp.einsum("phqk,pqhd->pkhd", grad_scores, queries, preferred_element_type=jnp.float32)
        * score_scale
    )
    return jnp.stack([grad_queries, grad_keys, grad_values], axis=2).astype(jnp.bfloat16)


def body(
    tokens,
    passage_lengths,
    cotangent,
    w_qkv,
    b_query,
    b_value,
    w_out,
    b_out,
    gain_one,
    shift_one,
    w_in,
    b_in,
    w_back,
    b_back,
    gain_two,
    shift_two,
):
    micro_count, own_rows, model_width = tokens.shape
    tp_count = lax.axis_size("tp")
    group_rows = own_rows * tp_count
    passages = passage_lengths.shape[1]
    passage_len = group_rows // passages
    local_width = w_qkv.shape[2]
    score_scale = 1.0 / math.sqrt(DH)
    row_start = lax.axis_index("tp") * own_rows
    positions = jnp.arange(passage_len, dtype=jnp.int32)
    row_ids = row_start + jnp.arange(own_rows, dtype=jnp.int32)
    passage_ids = jnp.arange(passages, dtype=jnp.int32)
    proj_weight = w_qkv.reshape(model_width, 3 * local_width)
    qkv_bias = jnp.stack([b_query, jnp.zeros_like(b_query), b_value])
    heads_used = local_width // DH
    in_weight, in_bias16, back_weight = (w_in, b_in, w_back)
    in_bias = in_bias16.astype(jnp.float32)
    ffn_cols = in_weight.shape[1]
    g_qkv = jnp.zeros((model_width, 3 * local_width), jnp.float32)
    g_query = jnp.zeros((local_width,), jnp.float32)
    g_value = jnp.zeros((local_width,), jnp.float32)
    g_out = jnp.zeros((local_width, model_width), jnp.float32)
    g_in = jnp.zeros((model_width, ffn_cols), jnp.float32)
    g_in_bias = jnp.zeros((ffn_cols,), jnp.float32)
    g_back = jnp.zeros((ffn_cols, model_width), jnp.float32)
    g_out_bias = jnp.zeros((model_width,), jnp.float32)
    g_gain_one = jnp.zeros((model_width,), jnp.float32)
    g_shift_one = jnp.zeros((model_width,), jnp.float32)
    g_back_bias = jnp.zeros((model_width,), jnp.float32)
    g_gain_two = jnp.zeros((model_width,), jnp.float32)
    g_shift_two = jnp.zeros((model_width,), jnp.float32)
    outputs = []
    input_grads = []
    for micro_step in range(micro_count):
        lengths = passage_lengths[micro_step]
        key_keep = positions[None, :] < lengths[:, None]
        own_len = jnp.sum(
            jnp.where(
                (row_ids // passage_len)[:, None] == passage_ids[None, :], lengths[None, :], 0
            ),
            axis=1,
        )
        own_keep = (row_ids % passage_len < own_len).astype(jnp.float32)
        token_own = tokens[micro_step]
        token_in = lax.all_gather(token_own, "tp", axis=0, tiled=True)
        projected = (
            jnp.dot(token_in, proj_weight, preferred_element_type=jnp.float32).reshape(
                group_rows, 3, local_width
            )
            + qkv_bias
        )
        qkv_blocks = projected.astype(jnp.bfloat16).reshape(
            group_rows // passage_len, passage_len, 3, heads_used, DH
        )
        context, log_total = attend_forward(qkv_blocks, key_keep, score_scale)
        context = context.reshape(group_rows, local_width)
        attn_out = lax.psum_scatter(
            jnp.dot(context, w_out, preferred_element_type=jnp.float32),
            "tp",
            scatter_dimension=0,
            tiled=True,
        )
        normed_one, unit_one, inverse_one = norm_forward(
            token_own.astype(jnp.float32) + attn_out + b_out, gain_one, shift_one
        )
        normed_low = normed_one.astype(jnp.bfloat16)
        hidden_rows = lax.all_gather(normed_low, "tp", axis=0, tiled=True)
        preact = jnp.dot(hidden_rows, in_weight, preferred_element_type=jnp.float32) + in_bias
        activation = jax.nn.gelu(preact, approximate=False).astype(jnp.bfloat16)
        ffn_out = lax.psum_scatter(
            jnp.dot(activation, back_weight, preferred_element_type=jnp.float32),
            "tp",
            scatter_dimension=0,
            tiled=True,
        )
        result, unit_two, inverse_two = norm_forward(
            normed_one + ffn_out + b_back, gain_two, shift_two
        )
        outputs.append(result.astype(jnp.bfloat16))
        grad_y = cotangent[micro_step].astype(jnp.float32) * own_keep[:, None]
        g_gain_two = g_gain_two + jnp.sum(grad_y * unit_two, axis=0)
        g_shift_two = g_shift_two + jnp.sum(grad_y, axis=0)
        grad_two = norm_backward(grad_y, unit_two, inverse_two, gain_two)
        g_back_bias = g_back_bias + jnp.sum(grad_two, axis=0)
        grad_ffn = grad_two.astype(jnp.bfloat16)
        grad_rows = lax.all_gather(grad_ffn, "tp", axis=0, tiled=True)
        g_back = g_back + jnp.einsum(
            "rf,rd->fd", activation, grad_rows, preferred_element_type=jnp.float32
        )
        grad_act = jnp.einsum(
            "rd,fd->rf", grad_rows, back_weight, preferred_element_type=jnp.float32
        )
        grad_preact = (grad_act * gelu_slope(preact)).astype(jnp.bfloat16)
        g_in_bias = g_in_bias + jnp.sum(grad_preact.astype(jnp.float32), axis=0)
        g_in = g_in + jnp.einsum(
            "rd,rf->df", hidden_rows, grad_preact, preferred_element_type=jnp.float32
        )
        grad_normed = lax.psum_scatter(
            jnp.einsum("rf,df->rd", grad_preact, in_weight, preferred_element_type=jnp.float32),
            "tp",
            scatter_dimension=0,
            tiled=True,
        )
        grad_one_in = grad_two + grad_normed
        g_gain_one = g_gain_one + jnp.sum(grad_one_in * unit_one, axis=0)
        g_shift_one = g_shift_one + jnp.sum(grad_one_in, axis=0)
        grad_one = norm_backward(grad_one_in, unit_one, inverse_one, gain_one)
        g_out_bias = g_out_bias + jnp.sum(grad_one, axis=0)
        grad_attn_rows = lax.all_gather(grad_one.astype(jnp.bfloat16), "tp", axis=0, tiled=True)
        g_out = g_out + jnp.einsum(
            "rc,rd->cd", context, grad_attn_rows, preferred_element_type=jnp.float32
        )
        grad_context = jnp.einsum(
            "rd,cd->rc", grad_attn_rows, w_out, preferred_element_type=jnp.float32
        ).astype(jnp.bfloat16)
        grad_blocks = attend_backward(
            qkv_blocks,
            key_keep,
            log_total,
            grad_context.reshape(group_rows // passage_len, passage_len, heads_used, DH),
            score_scale,
        )
        grad_split = grad_blocks.reshape(group_rows, 3, local_width)
        g_query = g_query + jnp.sum(grad_split[:, 0].astype(jnp.float32), axis=0)
        g_value = g_value + jnp.sum(grad_split[:, 2].astype(jnp.float32), axis=0)
        grad_flat = grad_split.reshape(group_rows, 3 * local_width)
        g_qkv = g_qkv + jnp.einsum(
            "rd,rc->dc", token_in, grad_flat, preferred_element_type=jnp.float32
        )
        input_grads.append(
            grad_one
            + lax.psum_scatter(
                jnp.einsum(
                    "rc,dc->rd", grad_flat, proj_weight, preferred_element_type=jnp.float32
                ).astype(jnp.bfloat16),
                "tp",
                scatter_dimension=0,
                tiled=True,
            ).astype(jnp.float32)
        )
    g_qkv, g_query, g_value, g_out, g_in, g_in_bias, g_back = lax.psum(
        (g_qkv, g_query, g_value, g_out, g_in, g_in_bias, g_back), "batch"
    )
    g_out_bias, g_gain_one, g_shift_one, g_back_bias, g_gain_two, g_shift_two = lax.psum(
        (g_out_bias, g_gain_one, g_shift_one, g_back_bias, g_gain_two, g_shift_two), ("batch", "tp")
    )
    return (
        jnp.stack(outputs),
        jnp.stack(input_grads),
        g_qkv.reshape(model_width, 3, local_width),
        g_query,
        g_value,
        g_out,
        g_out_bias,
        g_gain_one,
        g_shift_one,
        g_in,
        g_in_bias,
        g_back,
        g_back_bias,
        g_gain_two,
        g_shift_two,
    )


def solution(mesh):
    in_specs = (
        P(None, ("batch", "tp"), None),
        P(None, "batch"),
        P(None, ("batch", "tp"), None),
        P(None, None, "tp"),
        P("tp"),
        P("tp"),
        P("tp", None),
        P(),
        P(),
        P(),
        P(None, "tp"),
        P("tp"),
        P("tp", None),
        P(),
        P(),
        P(),
    )
    out_specs = (
        P(None, ("batch", "tp"), None),
        P(None, ("batch", "tp"), None),
        P(None, None, "tp"),
        P("tp"),
        P("tp"),
        P("tp", None),
        P(),
        P(),
        P(),
        P(None, "tp"),
        P("tp"),
        P("tp", None),
        P(),
        P(),
        P(),
    )
    return jax.shard_map(body, mesh=mesh, in_specs=in_specs, out_specs=out_specs, check_vma=False)
```

profile of v0, /device:TPU:16, one launch (start us, length us, event | category | flops | bytes accessed | tf_op | source)
XLA Modules:
  0.0 766.1 jit_solution(4249037735550400191)
XLA Ops:
  12.4 18.5 %all-gather.23.cloned.1.call-done = bf16[1,1024,768]{2,1,0:T(8,128)(2,1)} async-done(((bf16[1,256,768]{2,1,0:T(8,128)(2,1)}), bf16[1,1024,768]{2,1,0:T(8,128)(2,1)}) %all-gather.23.cloned.1.call-update) | async-done | bytes 1572880 | tf_op jit(solution)/shard_map/all_gather | solution.py:152
  41.8 10.8 %all-gather.25.cloned.1.call-done = bf16[1,1024,768]{2,1,0:T(8,128)(2,1)} async-done(((bf16[1,256,768]{2,1,0:T(8,128)(2,1)}), bf16[1,1024,768]{2,1,0:T(8,128)(2,1)}) %all-gather.25.cloned.1.call-update) | async-done | bytes 1572880 | tf_op jit(solution)/shard_map/all_gather | solution.py:152
  63.4 29.7 %reduce-scatter.9.cloned.1.call-done = f32[256,768]{1,0:T(8,128)} async-done(((f32[1024,768]{1,0:T(8,128)}), f32[256,768]{1,0:T(8,128)}) %reduce-scatter.9.cloned.1.call-update) | async-done | bytes 786448 | tf_op jit(solution)/shard_map/reduce_scatter | solution.py:164
  93.1 40.3 %reduce-scatter.13.cloned.1.call-done = f32[256,768]{1,0:T(8,128)} async-done(((f32[1024,768]{1,0:T(8,128)}), f32[256,768]{1,0:T(8,128)}) %reduce-scatter.13.cloned.1.call-update) | async-done | bytes 786448 | tf_op jit(solution)/shard_map/reduce_scatter | solution.py:164
  138.4 18.9 %all-gather.13.cloned.1.call-done = bf16[1024,768]{1,0:T(8,128)(2,1)} async-done(((bf16[256,768]{1,0:T(8,128)(2,1)}), bf16[1024,768]{1,0:T(8,128)(2,1)}) %all-gather.13.cloned.1.call-update) | async-done | bytes 1572880 | tf_op jit(solution)/shard_map/all_gather | solution.py:174
  157.3 4.5 fusion.114
  161.8 17.2 %all-gather.11.cloned.1.call-done = bf16[1024,768]{1,0:T(8,128)(2,1)} async-done(((bf16[256,768]{1,0:T(8,128)(2,1)}), bf16[1024,768]{1,0:T(8,128)(2,1)}) %all-gather.11.cloned.1.call-update) | async-done | bytes 1572880 | tf_op jit(solution)/shard_map/all_gather | solution.py:174
  179.0 16.8 %fusion.2 = (bf16[1024,768]{1,0:T(8,128)(2,1)S(1)}, bf16[1024,768]{1,0:T(8,128)(2,1)}, f32[1024,768]{1,0:T(8,128)}) fusion(f32[768]{0:T(1024)S(1)} %convert_element_type.183, f32[1024,768]{1,0:T(8,128)} %fusion.114, bf16[1024,768]{1,0:T(8,128)(2,1)} %all-gather.11.cloned.1.call-done, bf16[768,768]{1,0:T(8,128)(2,1)S(1)} %copy-done), kind=kOutput, calls=%fused_computation.6 | convolution fusion | flops 1311768576 | bytes 12192768 | tf_op jit(solution)/shard_map/dot_general | solution.py:175
  197.0 3.1 fusion.112
  200.1 4.8 fusion.115
  206.3 31.8 %reduce-scatter.11.cloned.1.call-done = f32[256,768]{1,0:T(8,128)} async-done(((f32[1024,768]{1,0:T(8,128)}), f32[256,768]{1,0:T(8,128)}) %reduce-scatter.11.cloned.1.call-update) | async-done | bytes 786448 | tf_op jit(solution)/shard_map/reduce_scatter | solution.py:177
  238.1 40.5 %reduce-scatter.15.cloned.1.call-done = f32[256,768]{1,0:T(8,128)} async-done(((f32[1024,768]{1,0:T(8,128)}), f32[256,768]{1,0:T(8,128)}) %reduce-scatter.15.cloned.1.call-update) | async-done | bytes 786448 | tf_op jit(solution)/shard_map/reduce_scatter | solution.py:177
  288.9 17.5 %all-gather.15.cloned.1.call-done = bf16[1024,768]{1,0:T(8,128)(2,1)} async-done(((bf16[256,768]{1,0:T(8,128)(2,1)}), bf16[1024,768]{1,0:T(8,128)(2,1)}) %all-gather.15.cloned.1.call-update) | async-done | bytes 1572880 | tf_op jit(solution)/shard_map/all_gather | solution.py:193
  306.4 5.4 convert_reduce_fusion.1
  313.0 3.1 fusion.116
  316.1 11.9 %all-gather.19.cloned.1.call-done = bf16[1024,768]{1,0:T(8,128)(2,1)} async-done(((bf16[256,768]{1,0:T(8,128)(2,1)}), bf16[1024,768]{1,0:T(8,128)(2,1)}) %all-gather.19.cloned.1.call-update) | async-done | bytes 1572880 | tf_op jit(solution)/shard_map/all_gather | solution.py:193
  328.1 5.4 convert_reduce_fusion
  334.6 3.1 fusion.117
  337.8 30.7 %reduce-scatter.17.cloned.1.call-done = f32[256,768]{1,0:T(8,128)} async-done(((f32[1024,768]{1,0:T(8,128)}), f32[256,768]{1,0:T(8,128)}) %reduce-scatter.17.cloned.1.call-update) | async-done | bytes 786448 | tf_op jit(solution)/shard_map/reduce_scatter | solution.py:205
  368.5 2.9 multiply_reduce_fusion.3
  372.6 36.2 %reduce-scatter.21.cloned.1.call-done = f32[256,768]{1,0:T(8,128)} async-done(((f32[1024,768]{1,0:T(8,128)}), f32[256,768]{1,0:T(8,128)}) %reduce-scatter.21.cloned.1.call-update) | async-done | bytes 786448 | tf_op jit(solution)/shard_map/reduce_scatter | solution.py:205
  408.8 3.0 fusion.99
  415.7 17.7 %all-gather.21.cloned.1.call-done = bf16[1024,768]{1,0:T(8,128)(2,1)} async-done(((bf16[256,768]{1,0:T(8,128)(2,1)}), bf16[1024,768]{1,0:T(8,128)(2,1)}) %all-gather.21.cloned.1.call-update) | async-done | bytes 1572880 | tf_op jit(solution)/shard_map/all_gather | solution.py:216
  437.5 2.9 multiply_reduce_fusion
  449.6 5.4 all-gather.17.cloned.1.call-done
  471.3 3.5 fusion.120
  476.7 2.9 convolution_add_fusion
  479.6 2.9 convolution_add_fusion.1
  495.1 40.4 %all-reduce = (f32[768]{0:T(1024)}, f32[768]{0:T(1024)}, f32[768]{0:T(1024)}, f32[768]{0:T(1024)}, f32[768]{0:T(1024)}, /*index=5*/f32[768]{0:T(1024)}) all-reduce(f32[768]{0:T(1024)S(1)} %add.332, f32[768]{0:T(1024)S(1)} %add.333, f32[768]{0:T(1024)S(1)} %add.334, ...), channel_id=1, replica_groups=mesh['batch'=8,'tp'=4] {'batch','tp'}, use_global_device_ids=true, to_apply=%region_42.43 | all-reduce | flops 4608 | bytes 36864 | tf_op jit(solution)/shard_map/psum | solution.py:251
  537.1 20.1 %all-reduce.1 = (f32[192]{0:T(256)}, f32[192]{0:T(256)}, f32[768]{0:T(1024)}) all-reduce(f32[192]{0:T(256)S(1)} %reshape.318, f32[192]{0:T(256)S(1)} %reshape.319, f32[768]{0:T(1024)S(1)} %add.336), channel_id=1, replica_groups=mesh['batch'=8,'tp'=4] {'batch'}, use_global_device_ids=true, to_apply=%region_35.36 | all-reduce | flops 1152 | bytes 9216 | tf_op jit(solution)/shard_map/psum | solution.py:248
  560.6 192.2 %all-reduce.5.cloned.1.call-done = (f32[768,3,192]{0,2,1:T(8,128)}, f32[192,768]{1,0:T(8,128)}, f32[768,768]{1,0:T(8,128)}, f32[768,768]{1,0:T(8,128)}) async-done(((f32[768,3,192]{0,2,1:T(8,128)}, f32[192,768]{1,0:T(8,128)}, f32[768,768]{1,0:T(8,128)}, f32[768,768]{1,0:T(8,128)}), (f32[768,3,192]{0,2,1:T(8,128)}, f32[192,768]{1,0:T(8,128)}, f32[768,768]{1,0:T(8,128)}, ...) | async-done | bytes 7077904 | tf_op jit(solution)/shard_map/psum | solution.py:248
  752.8 2.9 copy.165
  (291 shorter events, 103.9 us)
Async XLA Ops:
  7.2 150.1 %copy-start = (bf16[768,768]{1,0:T(8,128)(2,1)S(1)}, bf16[768,768]{1,0:T(8,128)(2,1)}, u32[]{:S(2)}) copy-start(bf16[768,768]{1,0:T(8,128)(2,1)} %param.26) | copy-start | bytes 3538948
  7.2 23.7 %all-gather.23.cloned.1.call-start = ((), (), s32[]{:S(2)}) async-start(), calls=%async_computation.22 | async-start | bytes 1966080 | tf_op jit(solution)/shard_map/all_gather | solution.py:152
  9.4 43.3 %all-gather.25.cloned.1.call-start = ((), (), s32[]{:S(2)}) async-start(), calls=%async_computation.23 | async-start | bytes 1966080 | tf_op jit(solution)/shard_map/all_gather | solution.py:152
  10.1 83.0 %reduce-scatter.9.cloned.1.call-start = ((), (), s32[]{:S(2)}) async-start(), calls=%async_computation.8 | async-start | bytes 3932160 | tf_op jit(solution)/shard_map/reduce_scatter | solution.py:164
  39.4 13.2 %copy-start.67 = (bf16[768,3,192]{0,2,1:T(8,128)(2,1)S(1)}, bf16[768,3,192]{0,2,1:T(8,128)(2,1)}, u32[]{:S(2)}) copy-start(bf16[768,3,192]{0,2,1:T(8,128)(2,1)} %param.19) | copy-start | bytes 2654212
  41.8 91.6 %reduce-scatter.13.cloned.1.call-start = ((), (), s32[]{:S(2)}) async-start(), calls=%async_computation.11 | async-start | bytes 3932160 | tf_op jit(solution)/shard_map/reduce_scatter | solution.py:164
  61.0 72.4 %copy-start.17 = (bf16[2,256,768]{2,1,0:T(8,128)(2,1)S(1)}, bf16[2,256,768]{2,1,0:T(8,128)(2,1)}, u32[]{:S(2)}) copy-start(bf16[2,256,768]{2,1,0:T(8,128)(2,1)} %param.16) | copy-start | bytes 2359300
  61.0 72.4 %copy-start.58 = (f32[768]{0:T(1024)S(1)}, f32[768]{0:T(1024)}, u32[]{:S(2)}) copy-start(f32[768]{0:T(1024)} %param.23) | copy-start | bytes 9220
  63.3 72.3 %copy-start.41 = (f32[768]{0:T(1024)S(1)}, f32[768]{0:T(1024)}, u32[]{:S(2)}) copy-start(f32[768]{0:T(1024)} %param.24) | copy-start | bytes 9220
  63.3 94.0 %all-gather.13.cloned.1.call-start = ((), (), s32[]{:S(2)}) async-start(), calls=%async_computation.12 | async-start | bytes 1966080 | tf_op jit(solution)/shard_map/all_gather | solution.py:174
  135.6 26.2 %copy-start.45 = (f32[256]{0:T(256)}, f32[256]{0:T(256)S(1)}, u32[]{:S(2)}) copy-start(f32[256]{0:T(256)S(1)} %add_rsqrt_fusion.3) | copy-start | bytes 3076
  137.5 41.4 %all-gather.11.cloned.1.call-start = ((), (), s32[]{:S(2)}) async-start(), calls=%async_computation.9 | async-start | bytes 1966080 | tf_op jit(solution)/shard_map/all_gather | solution.py:174
  138.1 100.0 %reduce-scatter.11.cloned.1.call-start = ((), (), s32[]{:S(2)}) async-start(), calls=%async_computation.10 | async-start | bytes 3932160 | tf_op jit(solution)/shard_map/reduce_scatter | solution.py:177
  138.4 40.6 %copy-start.57 = (f32[768]{0:T(1024)}, f32[768]{0:T(1024)S(1)}, u32[]{:S(2)}) copy-start(f32[768]{0:T(1024)S(1)} %convert_element_type.183) | copy-start | bytes 9220
  179.0 18.0 %copy-start.66 = (bf16[768,768]{1,0:T(8,128)(2,1)S(1)}, bf16[768,768]{1,0:T(8,128)(2,1)}, u32[]{:S(2)}) copy-start(bf16[768,768]{1,0:T(8,128)(2,1)} %param.28) | copy-start | bytes 3538948
  200.1 78.5 %reduce-scatter.15.cloned.1.call-start = ((), (), s32[]{:S(2)}) async-start(), calls=%async_computation.13 | async-start | bytes 3932160 | tf_op jit(solution)/shard_map/reduce_scatter | solution.py:177
  204.9 101.5 %all-gather.15.cloned.1.call-start = ((), (), s32[]{:S(2)}) async-start(), calls=%async_computation.14 | async-start | bytes 1966080 | tf_op jit(solution)/shard_map/all_gather | solution.py:193
  206.3 74.8 %copy-start.18 = (bf16[2,256,768]{2,1,0:T(8,128)(2,1)S(1)}, bf16[2,256,768]{2,1,0:T(8,128)(2,1)}, u32[]{:S(2)}) copy-start(bf16[2,256,768]{2,1,0:T(8,128)(2,1)} %param.18) | copy-start | bytes 2359300
  286.6 41.4 %all-gather.19.cloned.1.call-start = ((), (), s32[]{:S(2)}) async-start(), calls=%async_computation.18 | async-start | bytes 1966080 | tf_op jit(solution)/shard_map/all_gather | solution.py:193
  288.6 79.9 %reduce-scatter.17.cloned.1.call-start = ((), (), s32[]{:S(2)}) async-start(), calls=%async_computation.15 | async-start | bytes 3932160 | tf_op jit(solution)/shard_map/reduce_scatter | solution.py:205
  316.1 92.8 %reduce-scatter.21.cloned.1.call-start = ((), (), s32[]{:S(2)}) async-start(), calls=%async_computation.19 | async-start | bytes 3932160 | tf_op jit(solution)/shard_map/reduce_scatter | solution.py:205
  337.8 95.5 %all-gather.21.cloned.1.call-start = ((), (), s32[]{:S(2)}) async-start(), calls=%async_computation.20 | async-start | bytes 1966080 | tf_op jit(solution)/shard_map/all_gather | solution.py:216
  412.7 24.7 %copy-start.25 = (bf16[4,256,1,3,64]{1,0,4,3,2:T(4,128)(2,1)S(1)}, bf16[4,256,1,3,64]{1,0,4,3,2:T(4,128)(2,1)}, u32[]{:S(2)}) copy-start(bf16[4,256,1,3,64]{1,0,4,3,2:T(4,128)(2,1)} %copy-done.24) | copy-start | bytes 1179652
  413.5 41.4 %all-gather.17.cloned.1.call-start = ((), (), s32[]{:S(2)}) async-start(), calls=%async_computation.16 | async-start | bytes 1966080 | tf_op jit(solution)/shard_map/all_gather | solution.py:216
  415.1 142.0 %reduce-scatter.23.cloned.1.call-start = ((), (), s32[]{:S(2)}) async-start(), calls=%async_computation.21 | async-start | bytes 1966080 | tf_op jit(solution)/shard_map/reduce_scatter | solution.py:239
  446.7 8.2 %copy-start.36 = (bf16[192,768]{1,0:T(8,128)(2,1)S(1)}, bf16[192,768]{1,0:T(8,128)(2,1)}, u32[]{:S(2)}) copy-start(bf16[192,768]{1,0:T(8,128)(2,1)} %param.22) | copy-start | bytes 884740
  449.3 9.8 %copy-start.23 = (bf16[4,256,1,3,64]{1,0,4,3,2:T(4,128)(2,1)S(1)}, bf16[4,256,1,3,64]{1,0,4,3,2:T(4,128)(2,1)}, u32[]{:S(2)}) copy-start(bf16[4,256,1,3,64]{1,0,4,3,2:T(4,128)(2,1)} %copy-done.22) | copy-start | bytes 1179652
  449.3 108.9 %reduce-scatter.19.cloned.1.call-start = ((), (), s32[]{:S(2)}) async-start(), calls=%async_computation.17 | async-start | bytes 1966080 | tf_op jit(solution)/shard_map/reduce_scatter | solution.py:239
  471.0 281.8 %all-reduce.5.cloned.1.call-start = ((), (), s32[]{:S(2)}) async-start(), calls=%async_computation.24 | async-start | bytes 14155776 | tf_op jit(solution)/shard_map/psum | solution.py:248
  471.3 3.5 copy-start.64
  471.3 3.5 copy-start.75
  752.8 3.8 copy-start.21
  (61 other events, 112.0 us)
Sparse Core Ops, SparseCore 0:
  10.1 20.6 all-gather.22
  33.0 19.6 all-gather.24
  55.2 37.8 reduce-scatter.8
  95.5 37.8 reduce-scatter.12
  137.6 19.6 all-gather.12
  159.3 19.6 all-gather.10
  200.2 37.8 reduce-scatter.10
  240.6 37.8 reduce-scatter.14
  286.8 19.6 all-gather.14
  308.4 19.6 all-gather.18
  330.6 37.8 reduce-scatter.16
  370.9 37.8 reduce-scatter.20
  413.6 19.6 all-gather.20
  435.3 19.6 all-gather.16
  457.4 27.9 reduce-scatter.22
  487.8 28.1 reduce-scatter.18
  521.4 231.3 all-reduce.4
where the time goes:
time: 777 us; the launch traced here: 766 us
  waiting for transfers between devices  521 us (67%)
  matrix products  97.8 us (13%)
  blocking collectives  60.5 us (8%)
  other arithmetic  38 us (5%)
  local copies, waits for them, and re-layouts  32 us (4%)
  between operations  15.1 us (2%)
    psum x1, waiting for transfers between devices, body(): lax.psum((g_qkv, g_query, g_value, g_out, g_in, g_in_bias, g_back), 'batch')  192 us
    reduce_scatter x2, waiting for transfers between devices, body(): lax.psum_scatter(jnp.dot(activation, back_weight, preferred_element_type=...  72.3 us
    reduce_scatter x2, waiting for transfers between devices, body(): lax.psum_scatter(jnp.dot(context, w_out, preferred_element_type=jnp.float...  70 us
    reduce_scatter x2, waiting for transfers between devices, body(): lax.psum_scatter(jnp.einsum('rf,df->rd', grad_preact, in_weight, preferre...  66.9 us
    psum x1, blocking collectives, body(): lax.psum((g_out_bias, g_gain_one, g_shift_one, g_back_bias, g_gain_two, g...  40.4 us
    all_gather x2, waiting for transfers between devices, body(): hidden_rows = lax.all_gather(normed_low, 'tp', axis=0, tiled=True)  36.1 us
    all_gather x2, waiting for transfers between devices, body(): grad_rows = lax.all_gather(grad_ffn, 'tp', axis=0, tiled=True)  29.4 us
    all_gather x2, waiting for transfers between devices, body(): token_in = lax.all_gather(token_own, 'tp', axis=0, tiled=True)  29.3 us
  transfers between devices with their start and end apart: 17, of which 15 were waited for; matrix products, arithmetic and copies ran while one was open for 14% of the time, Pallas kernels for 0%

commit v1 on v0

v1 whole, which is shorter than its diff:
```python
import math

import jax
import jax.numpy as jnp
from jax import lax
from jax.sharding import PartitionSpec as P

DH = 64
AXES = ("batch", "tp")
epsilon = 1e-05
F32 = jnp.float32
BF16 = jnp.bfloat16


def norm_forward(values_in, gain_vec, shift_vec):
    middle = jnp.mean(values_in, axis=-1, keepdims=True)
    centred = values_in - middle
    spread = jnp.mean(centred * centred, axis=-1, keepdims=True)
    inverse = lax.rsqrt(spread + epsilon)
    unit_rows = centred * inverse
    return (unit_rows * gain_vec + shift_vec, unit_rows, inverse)


def norm_backward(grad_rows, unit_rows, inverse, gain_vec):
    scaled = grad_rows * gain_vec
    mean_one = jnp.mean(scaled, axis=-1, keepdims=True)
    mean_two = jnp.mean(scaled * unit_rows, axis=-1, keepdims=True)
    return inverse * (scaled - mean_one - unit_rows * mean_two)


def gelu_slope(preact):
    normal_cdf = 0.5 * (1.0 + lax.erf(preact * (1.0 / math.sqrt(2.0))))
    density = jnp.exp(-0.5 * preact * preact) * (1.0 / math.sqrt(2.0 * math.pi))
    return normal_cdf + preact * density


def attend_forward(qkv_blocks, key_keep, score_scale):
    queries = qkv_blocks[:, :, 0]
    key_rows = qkv_blocks[:, :, 1]
    value_rows = qkv_blocks[:, :, 2]
    scores = (
        jnp.einsum("pqhd,pkhd->phqk", queries, key_rows, preferred_element_type=F32)
        * score_scale
    )
    scores = jnp.where(key_keep[:, None, None, :], scores, -1000000000.0)
    row_max = jnp.max(scores, axis=-1, keepdims=True)
    exponent = jnp.exp(scores - row_max)
    row_total = jnp.sum(exponent, axis=-1, keepdims=True)
    attn_probs = exponent / row_total
    log_total = row_max + jnp.log(row_total)
    context = jnp.einsum(
        "phqk,pkhd->pqhd", attn_probs.astype(BF16), value_rows, preferred_element_type=F32
    )
    return (context.astype(BF16), log_total)


def attend_backward(qkv_blocks, key_keep, log_total, grad_context, score_scale):
    queries = qkv_blocks[:, :, 0]
    key_rows = qkv_blocks[:, :, 1]
    value_rows = qkv_blocks[:, :, 2]
    scores = (
        jnp.einsum("pqhd,pkhd->phqk", queries, key_rows, preferred_element_type=F32)
        * score_scale
    )
    scores = jnp.where(key_keep[:, None, None, :], scores, -1000000000.0)
    attn_probs = jnp.exp(scores - log_total)
    grad_values = jnp.einsum(
        "phqk,pqhd->pkhd", attn_probs.astype(BF16), grad_context, preferred_element_type=F32
    )
    grad_probs = jnp.einsum(
        "pqhd,pkhd->phqk", grad_context, value_rows, preferred_element_type=F32
    )
    row_delta = jnp.sum(attn_probs * grad_probs, axis=-1, keepdims=True)
    grad_scores = (attn_probs * (grad_probs - row_delta)).astype(BF16)
    grad_queries = (
        jnp.einsum("phqk,pkhd->pqhd", grad_scores, key_rows, preferred_element_type=F32)
        * score_scale
    )
    grad_keys = (
        jnp.einsum("phqk,pqhd->pkhd", grad_scores, queries, preferred_element_type=F32)
        * score_scale
    )
    return jnp.stack([grad_queries, grad_keys, grad_values], axis=2).astype(BF16)


def flat_perm(move):
    pairs = []
    for z in range(4):
        for y in range(2):
            for x in range(2):
                for c in range(2):
                    to = move(z, y, x, c)
                    if to is not None:
                        z2, y2, x2, c2 = to
                        pairs.append(
                            (((z * 2 + y) * 2 + x) * 2 + c, ((z2 * 2 + y2) * 2 + x2) * 2 + c2)
                        )
    return pairs


class GridMoves:
    def __init__(self):
        self.row = lax.axis_index("batch") % 2
        self.layer = lax.axis_index("batch") // 2
        self.outer = (self.layer == 0) | (self.layer == 3)
        self.to_core = flat_perm(lambda z, y, x, c: (z, y, x, 1 - c))
        self.to_x = flat_perm(lambda z, y, x, c: (z, y, 1 - x, c))
        self.to_y = flat_perm(lambda z, y, x, c: (z, 1 - y, x, c))
        self.to_inner = flat_perm(
            lambda z, y, x, c: {0: (1, y, x, c), 3: (2, y, x, c)}.get(z)
        )
        self.across = flat_perm(
            lambda z, y, x, c: {1: (2, y, x, c), 2: (1, y, x, c)}.get(z)
        )
        self.to_outer = flat_perm(
            lambda z, y, x, c: {1: (0, y, x, c), 2: (3, y, x, c)}.get(z)
        )

    def send(self, value, pairs):
        return lax.ppermute(value, AXES, pairs)

    def half(self, value, which):
        rows = value.shape[0] // 2
        return lax.dynamic_slice_in_dim(value, which * rows, rows, axis=0)

    def order(self, mine, other):
        return jnp.where(
            self.row == 0,
            jnp.concatenate([mine, other], axis=0),
            jnp.concatenate([other, mine], axis=0),
        )

    def gather(self, own):
        first = self.send(self.half(own, self.row), self.to_x)
        second = self.send(first, self.to_y)
        far = self.order(first, second)
        return [own, self.send(own, self.to_core), far, self.send(far, self.to_core)]

    def gather_small(self, own):
        pair = jnp.stack([own, self.send(own, self.to_core)])
        far = self.send(pair, self.to_x)
        return [pair[0], pair[1], far[0], far[1]]

    def add(self, one, two):
        return (one.astype(F32) + two.astype(F32)).astype(BF16)

    def reduce(self, parts):
        low = [part.astype(BF16) for part in parts]
        got = self.send(jnp.stack([low[1], low[3]]), self.to_core)
        far = (parts[2] + got[1].astype(F32)).astype(BF16)
        near = (parts[0] + got[0].astype(F32)).astype(BF16)
        got = self.send(far, self.to_x)
        pass_on = self.add(self.half(near, 1 - self.row), self.half(got, 1 - self.row))
        keep = self.add(self.half(near, self.row), self.half(got, self.row))
        keep = self.add(keep, self.send(pass_on, self.to_y))
        keep = self.add(keep, self.send(keep, self.to_inner))
        keep = self.add(keep, self.send(keep, self.across))
        keep = jnp.where(self.outer, self.send(keep, self.to_outer), keep)
        other = self.send(keep, self.to_y)
        return self.order(keep, other).astype(F32)

    def reduce_all(self, value):
        for pairs in (self.to_core, self.to_x, self.to_y, self.to_inner, self.across):
            value = value + self.send(value, pairs)
        return jnp.where(self.outer, self.send(value, self.to_outer), value)


class PlainMoves:
    def gather(self, own):
        whole = lax.all_gather(own, "tp", axis=0)
        return [whole[i] for i in range(whole.shape[0])]

    gather_small = gather

    def reduce(self, parts):
        mine = lax.psum_scatter(jnp.stack(parts), "tp", scatter_dimension=0, tiled=False)
        return lax.psum(mine, "batch")

    def reduce_all(self, value):
        return lax.psum(value, AXES)

def body(
    tokens,
    passage_lengths,
    cotangent,
    w_qkv,
    b_query,
    b_value,
    w_out,
    b_out,
    gain_one,
    shift_one,
    w_in,
    b_in,
    w_back,
    b_back,
    gain_two,
    shift_two,
):
    micro_count, own_rows, model_width = tokens.shape
    tp_count = lax.axis_size("tp")
    batch_count = lax.axis_size("batch")
    passage_len = own_rows * tp_count // passage_lengths.shape[1]
    own_passages = own_rows // passage_len
    assert own_passages * passage_len == own_rows
    grid = (batch_count, tp_count) == (8, 4)
    moves = GridMoves() if grid else PlainMoves()
    width = w_qkv.shape[2]
    heads = width // DH
    units = w_in.shape[1]
    score_scale = 1.0 / math.sqrt(DH)
    rows = micro_count * own_rows
    position = lax.axis_index("tp")

    small = jnp.concatenate([b_query, b_value, b_in.astype(F32)])
    small_parts = moves.gather_small(small)
    qkv_parts = moves.gather(w_qkv.reshape(model_width, 3 * width))
    out_parts = moves.gather(w_out)
    in_parts = moves.gather(w_in)
    back_parts = moves.gather(w_back)

    lengths = lax.dynamic_slice_in_dim(
        passage_lengths, position * own_passages, own_passages, axis=1
    ).reshape(micro_count * own_passages)
    slots = jnp.arange(passage_len, dtype=jnp.int32)
    key_keep = slots[None, :] < lengths[:, None]
    keep_rows = key_keep.reshape(rows, 1).astype(F32)
    x = tokens.reshape(rows, model_width)
    dy = cotangent.reshape(rows, model_width)

    qkv_rows, contexts, log_totals = [], [], []
    attn_out = 0.0
    for part in range(tp_count):
        bias_q = small_parts[part][:width]
        bias_v = small_parts[part][width : 2 * width]
        bias = jnp.concatenate([bias_q, jnp.zeros_like(bias_q), bias_v])
        projected = (
            jnp.dot(x, qkv_parts[part], preferred_element_type=F32) + bias
        ).astype(BF16)
        blocks = projected.reshape(-1, passage_len, 3, heads, DH)
        context, log_total = attend_forward(blocks, key_keep, score_scale)
        context = context.reshape(rows, width)
        qkv_rows.append(blocks)
        contexts.append(context)
        log_totals.append(log_total)
        attn_out = attn_out + jnp.dot(context, out_parts[part], preferred_element_type=F32)
    normed_one, unit_one, inverse_one = norm_forward(
        x.astype(F32) + attn_out + b_out, gain_one, shift_one
    )
    normed_low = normed_one.astype(BF16)
    preacts, activations = [], []
    ffn_out = 0.0
    for part in range(tp_count):
        preact = (
            jnp.dot(normed_low, in_parts[part], preferred_element_type=F32)
            + small_parts[part][2 * width :]
        )
        activation = jax.nn.gelu(preact, approximate=False).astype(BF16)
        preacts.append(preact)
        activations.append(activation)
        ffn_out = ffn_out + jnp.dot(activation, back_parts[part], preferred_element_type=F32)
    result, unit_two, inverse_two = norm_forward(normed_one + ffn_out + b_back, gain_two, shift_two)
    layer_out = result.astype(BF16).reshape(tokens.shape)

    grad_y = dy.astype(F32) * keep_rows
    g_gain_two = jnp.sum(grad_y * unit_two, axis=0)
    g_shift_two = jnp.sum(grad_y, axis=0)
    grad_two = norm_backward(grad_y, unit_two, inverse_two, gain_two)
    g_back_bias = jnp.sum(grad_two, axis=0)
    grad_ffn = grad_two.astype(BF16)
    g_back = moves.reduce(
        [
            jnp.einsum("rf,rd->fd", activations[part], grad_ffn, preferred_element_type=F32)
            for part in range(tp_count)
        ]
    )
    grad_preacts, g_in_bias = [], []
    grad_normed = grad_two
    for part in range(tp_count):
        grad_act = jnp.einsum(
            "rd,fd->rf", grad_ffn, back_parts[part], preferred_element_type=F32
        )
        grad_preact = (grad_act * gelu_slope(preacts[part])).astype(BF16)
        grad_preacts.append(grad_preact)
        g_in_bias.append(jnp.sum(grad_preact.astype(F32), axis=0))
    g_in = moves.reduce(
        [
            jnp.einsum("rd,rf->df", normed_low, grad_preacts[part], preferred_element_type=F32)
            for part in range(tp_count)
        ]
    )
    for part in range(tp_count):
        grad_normed = grad_normed + jnp.einsum(
            "rf,df->rd", grad_preacts[part], in_parts[part], preferred_element_type=F32
        )
    g_gain_one = jnp.sum(grad_normed * unit_one, axis=0)
    g_shift_one = jnp.sum(grad_normed, axis=0)
    grad_one = norm_backward(grad_normed, unit_one, inverse_one, gain_one)
    g_out_bias = jnp.sum(grad_one, axis=0)
    grad_attn = grad_one.astype(BF16)
    g_out = moves.reduce(
        [
            jnp.einsum("rc,rd->cd", contexts[part], grad_attn, preferred_element_type=F32)
            for part in range(tp_count)
        ]
    )
    grad_flats, g_query, g_value = [], [], []
    grad_x = grad_one
    for part in range(tp_count):
        grad_context = jnp.einsum(
            "rd,cd->rc", grad_attn, out_parts[part], preferred_element_type=F32
        ).astype(BF16)
        grad_blocks = attend_backward(
            qkv_rows[part],
            key_keep,
            log_totals[part],
            grad_context.reshape(-1, passage_len, heads, DH),
            score_scale,
        )
        grad_flat = grad_blocks.reshape(rows, 3 * width)
        grad_flats.append(grad_flat)
        sums = jnp.sum(grad_flat.astype(F32), axis=0)
        g_query.append(sums[:width])
        g_value.append(sums[2 * width :])
    g_qkv = moves.reduce(
        [
            jnp.einsum("rd,rc->dc", x, grad_flats[part], preferred_element_type=F32)
            for part in range(tp_count)
        ]
    )
    for part in range(tp_count):
        grad_x = grad_x + jnp.einsum(
            "rc,dc->rd", grad_flats[part], qkv_parts[part], preferred_element_type=F32
        )
    sharded = jnp.stack(
        [
            jnp.concatenate([g_query[part], g_value[part], g_in_bias[part]])
            for part in range(tp_count)
        ]
    )
    if grid:
        slots_of = jnp.bitwise_xor(jnp.arange(tp_count, dtype=jnp.int32), position)
        pick = (slots_of[:, None] == jnp.arange(tp_count, dtype=jnp.int32)[None, :]).astype(F32)
        sharded = jnp.sum(pick[:, :, None] * sharded[None, :, :], axis=1)
    common = jnp.concatenate(
        [g_out_bias, g_gain_one, g_shift_one, g_back_bias, g_gain_two, g_shift_two]
    )
    total = moves.reduce_all(jnp.concatenate([sharded.reshape(-1), common]))
    mine = lax.dynamic_slice_in_dim(
        total[: sharded.size].reshape(tp_count, -1), position, 1, axis=0
    )[0]
    tail = total[sharded.size :].reshape(6, model_width)
    return (
        layer_out,
        grad_x.reshape(tokens.shape),
        g_qkv.reshape(model_width, 3, width),
        mine[:width],
        mine[width : 2 * width],
        g_out,
        tail[0],
        tail[1],
        tail[2],
        g_in,
        mine[2 * width :],
        g_back,
        tail[3],
        tail[4],
        tail[5],
    )


def solution(mesh):
    in_specs = (
        P(None, ("batch", "tp"), None),
        P(None, "batch"),
        P(None, ("batch", "tp"), None),
        P(None, None, "tp"),
        P("tp"),
        P("tp"),
        P("tp", None),
        P(),
        P(),
        P(),
        P(None, "tp"),
        P("tp"),
        P("tp", None),
        P(),
        P(),
        P(),
    )
    out_specs = (
        P(None, ("batch", "tp"), None),
        P(None, ("batch", "tp"), None),
        P(None, None, "tp"),
        P("tp"),
        P("tp"),
        P("tp", None),
        P(),
        P(),
        P(),
        P(None, "tp"),
        P("tp"),
        P("tp", None),
        P(),
        P(),
        P(),
    )
    return jax.shard_map(body, mesh=mesh, in_specs=in_specs, out_specs=out_specs, check_vma=False)
```

time: 777 us -> 443 us (0.57)
  waiting for transfers between devices: 521 us -> 177 us
  blocking collectives: 60.5 us -> 0 us
  starting transfers between devices: 2.01 us -> 56.4 us
  matrix products: 97.8 us -> 125 us
  local copies, waits for them, and re-layouts: 32 us -> 46 us
  between operations: 15.1 us -> 2.77 us
  other arithmetic: 38 us -> 29.8 us
    reduce_scatter x8 -> x0, waiting for transfers between devices: 209 us -> none  [the longest x2 72.3 us: body(): lax.psum_scatter(jnp.dot(activation, back_weight, preferred_element_type=...]
    psum x1 -> x0, waiting for transfers between devices: 192 us -> none  [body(): lax.psum((g_qkv, g_query, g_value, g_out, g_in, g_in_bias, g_back), 'batch')]
    ppermute x0 -> x52, waiting for transfers between devices: none -> 177 us  [send(): return lax.ppermute(value, AXES, pairs)]
    all_gather x8 -> x0, waiting for transfers between devices: 118 us -> none  [the longest x2 36.1 us: body(): hidden_rows = lax.all_gather(normed_low, 'tp', axis=0, tiled=True)]
    psum x2 -> x0, blocking collectives: 60.5 us -> none  [the longest x1 40.4 us: body(): lax.psum((g_out_bias, g_gain_one, g_shift_one, g_back_bias, g_gain_two, g...]
    ppermute x0 -> x52, starting transfers between devices: none -> 56.4 us  [send(): return lax.ppermute(value, AXES, pairs)]
    dot_general x30 -> x60, matrix products: 88.6 us -> 114 us  [the longest x4 22.8 us: body(): jnp.dot(normed_low, in_parts[part], preferred_element_type=F32)]
    reduce_sum x8 -> x9, other arithmetic: 15.2 us -> 4.05 us  [the longest x1 1.62 us: body(): g_back_bias = jnp.sum(grad_two, axis=0)]
  transfers between devices with their start and end apart: 17 -> 52, of which waited for: 15 -> 19; matrix products, arithmetic and copies ran while one was open for 14% -> 25% of each run, Pallas kernels for 0% -> 0%
where the time goes in v1:
time: 443 us; the launch traced here: 436 us
  waiting for transfers between devices  177 us (40%)
  matrix products  125 us (28%)
  starting transfers between devices  56.4 us (13%)
  local copies, waits for them, and re-layouts  46 us (10%)
  other arithmetic  29.8 us (7%)
    ppermute x52, waiting for transfers between devices, send(): return lax.ppermute(value, AXES, pairs)  177 us
    ppermute x52, starting transfers between devices, send(): return lax.ppermute(value, AXES, pairs)  56.4 us
    dot_general x4, matrix products, body(): jnp.dot(normed_low, in_parts[part], preferred_element_type=F32)  22.8 us
    dot_general x4, matrix products, body(): jnp.einsum('rd,fd->rf', grad_ffn, back_parts[part], preferred_element_typ...  11.2 us
    unnamed x228, local copies, waits for them, and re-layouts  10.7 us
    dot_general x4, matrix products, body(): jnp.einsum('rf,df->rd', grad_preacts[part], in_parts[part], preferred_ele...  10 us
    dot_general x4, matrix products, body(): jnp.dot(activation, back_parts[part], preferred_element_type=F32)  9.61 us
  transfers between devices with their start and end apart: 52, of which 19 were waited for; matrix products, arithmetic and copies ran while one was open for 25% of the time, Pallas kernels for 0%

profile of v1, /device:TPU:16, one launch (start us, length us, event | category | flops | bytes accessed | tf_op | source)
XLA Modules:
  0.0 436.5 jit_solution(13947979280929827899)
XLA Ops:
  15.1 17.2 %collective-permute-done.5 = f32[2,1152]{1,0:T(2,128)S(1)} collective-permute-done((f32[2,1152]{1,0:T(2,128)S(1)}, f32[2,1152]{1,0:T(2,128)S(1)}, u32[]{:S(2)}, u32[]{:S(2)}) %collective-permute-start.5) | collective-permute-done | bytes 9248 | tf_op jit(solution)/shard_map/ppermute | solution.py:120
  41.8 4.9 %collective-permute-done.7 = bf16[96,768]{1,0:T(8,128)(2,1)S(1)} collective-permute-done((bf16[96,768]{1,0:T(8,128)(2,1)}, bf16[96,768]{1,0:T(8,128)(2,1)S(1)}, u32[]{:S(2)}, u32[]{:S(2)}) %collective-permute-start.7) | collective-permute-done | bytes 147488 | tf_op jit(solution)/shard_map/ppermute | solution.py:120
  49.9 6.3 %collective-permute-done.4 = bf16[384,576]{0,1:T(8,128)(2,1)S(1)} collective-permute-done((bf16[384,576]{0,1:T(8,128)(2,1)}, bf16[384,576]{0,1:T(8,128)(2,1)S(1)}, u32[]{:S(2)}, u32[]{:S(2)}) %collective-permute-start.4) | collective-permute-done | bytes 442400 | tf_op jit(solution)/shard_map/ppermute | solution.py:120
  61.5 2.9 reshape.377
  82.2 2.9 maximum_select_fusion
  85.6 3.0 maximum_select_fusion.1
  101.4 6.0 %fusion.8 = (bf16[512,768]{1,0:T(8,128)(2,1)S(1)}, f32[512,768]{1,0:T(8,128)S(1)}) fusion(f32[768]{0:T(1024)S(1)} %convert_element_type.552, bf16[512,768]{1,0:T(8,128)(2,1)S(1)} %fusion.80, bf16[768,768]{1,0:T(8,128)(2,1)} %param.26), kind=kOutput, calls=%fused_computation.25 | convolution fusion | flops 629932032 | bytes 4328448 | tf_op jit(solution)/shard_map/dot_general | solution.py:255
  109.8 5.5 %fusion.11 = (bf16[512,768]{1,0:T(8,128)(2,1)S(1)}, f32[512,768]{1,0:T(8,128)S(1)}) fusion(f32[768]{0:T(1024)S(1)} %copy-done.97, bf16[512,768]{1,0:T(8,128)(2,1)S(1)} %fusion.80, bf16[768,768]{1,0:T(8,128)(2,1)} %collective-permute-done.10), kind=kOutput, calls=%fused_computation.28 | convolution fusion | flops 629932032 | bytes 4328448 | tf_op jit(solution)/shard_map/dot_general | solution.py:255
  117.6 5.4 %fusion.14 = (bf16[512,768]{1,0:T(8,128)(2,1)S(1)}, f32[512,768]{1,0:T(8,128)S(1)}) fusion(f32[768]{0:T(1024)S(1)} %get-tuple-element.23, bf16[512,768]{1,0:T(8,128)(2,1)S(1)} %fusion.80, bf16[768,768]{1,0:T(8,128)(2,1)} %maximum_select_fusion), kind=kOutput, calls=%fused_computation.31 | convolution fusion | flops 629932032 | bytes 4328448 | tf_op jit(solution)/shard_map/dot_general | solution.py:255
  123.1 5.9 %fusion.17 = (bf16[512,768]{1,0:T(8,128)(2,1)S(1)}, f32[512,768]{1,0:T(8,128)S(1)}) fusion(f32[768]{0:T(1024)S(1)} %get-tuple-element.24, bf16[512,768]{1,0:T(8,128)(2,1)S(1)} %fusion.80, bf16[768,768]{1,0:T(8,128)(2,1)} %collective-permute-done.16), kind=kOutput, calls=%fused_computation.34 | convolution fusion | flops 629932032 | bytes 4328448 | tf_op jit(solution)/shard_map/dot_general | solution.py:255
  139.4 2.7 convert_reduce_fusion.3
  144.5 3.0 convert_reduce_fusion
  149.9 3.0 convert_reduce_fusion.2
  155.2 2.9 multiply_reduce_fusion.1
  163.6 2.7 convolution_bitcast_fusion
  173.4 2.7 convolution_bitcast_fusion.2
  237.1 3.9 collective-permute-done.28
  254.2 66.5 %collective-permute-done.32 = bf16[192,768]{1,0:T(8,128)(2,1)S(1)} collective-permute-done((bf16[192,768]{1,0:T(8,128)(2,1)S(1)}, bf16[192,768]{1,0:T(8,128)(2,1)S(1)}, u32[]{:S(2)}, u32[]{:S(2)}) %collective-permute-start.32) | collective-permute-done | bytes 294944 | tf_op jit(solution)/shard_map/ppermute | solution.py:120
  328.8 8.1 %collective-permute-done.20 = bf16[384,576]{0,1:T(8,128)(2,1)S(1)} collective-permute-done((bf16[384,576]{0,1:T(8,128)(2,1)S(1)}, bf16[384,576]{0,1:T(8,128)(2,1)S(1)}, u32[]{:S(2)}, u32[]{:S(2)}) %collective-permute-start.20) | collective-permute-done | bytes 442400 | tf_op jit(solution)/shard_map/ppermute | solution.py:120
  338.4 11.2 %collective-permute-done.40 = bf16[384,768]{1,0:T(8,128)(2,1)S(1)} collective-permute-done((bf16[384,768]{1,0:T(8,128)(2,1)S(1)}, bf16[384,768]{1,0:T(8,128)(2,1)S(1)}, u32[]{:S(2)}, u32[]{:S(2)}) %collective-permute-start.40) | collective-permute-done | bytes 589856 | tf_op jit(solution)/shard_map/ppermute | solution.py:120
  351.1 5.7 %collective-permute-done.47 = bf16[384,768]{1,0:T(8,128)(2,1)S(1)} collective-permute-done((bf16[384,768]{1,0:T(8,128)(2,1)S(1)}, bf16[384,768]{1,0:T(8,128)(2,1)S(1)}, u32[]{:S(2)}, u32[]{:S(2)}) %collective-permute-start.47) | collective-permute-done | bytes 589856 | tf_op jit(solution)/shard_map/ppermute | solution.py:120
  358.5 3.5 collective-permute-start.35
  367.0 3.5 collective-permute-start.42
  370.5 3.7 collective-permute-done.48
  374.4 3.5 collective-permute-start.49
  380.7 8.9 %collective-permute-done.42 = bf16[384,768]{1,0:T(8,128)(2,1)S(1)} collective-permute-done((bf16[384,768]{1,0:T(8,128)(2,1)S(1)}, bf16[384,768]{1,0:T(8,128)(2,1)S(1)}, u32[]{:S(2)}, u32[]{:S(2)}) %collective-permute-start.42) | collective-permute-done | bytes 589856 | tf_op jit(solution)/shard_map/ppermute | solution.py:120
  391.2 6.2 %collective-permute-done.49 = bf16[384,768]{1,0:T(8,128)(2,1)S(1)} collective-permute-done((bf16[384,768]{1,0:T(8,128)(2,1)S(1)}, bf16[384,768]{1,0:T(8,128)(2,1)S(1)}, u32[]{:S(2)}, u32[]{:S(2)}) %collective-permute-start.49) | collective-permute-done | bytes 589856 | tf_op jit(solution)/shard_map/ppermute | solution.py:120
  401.1 3.4 collective-permute-done.43
  405.2 6.9 %collective-permute-done.50 = bf16[384,768]{1,0:T(8,128)(2,1)S(1)} collective-permute-done((bf16[384,768]{1,0:T(8,128)(2,1)S(1)}, bf16[384,768]{1,0:T(8,128)(2,1)S(1)}, u32[]{:S(2)}, u32[]{:S(2)}) %collective-permute-start.50) | collective-permute-done | bytes 589856 | tf_op jit(solution)/shard_map/ppermute | solution.py:120
  418.0 10.0 %collective-permute-done.44 = bf16[384,768]{1,0:T(8,128)(2,1)} collective-permute-done((bf16[384,768]{1,0:T(8,128)(2,1)S(1)}, bf16[384,768]{1,0:T(8,128)(2,1)}, u32[]{:S(2)}, u32[]{:S(2)}) %collective-permute-start.44) | collective-permute-done | bytes 589856 | tf_op jit(solution)/shard_map/ppermute | solution.py:120
  427.9 2.9 fusion.99
  430.8 3.9 collective-permute-done.51
  (511 shorter events, 205.2 us)
Async XLA Ops:
  1.6 65.1 %collective-permute-start = (bf16[768,576]{0,1:T(8,128)(2,1)}, bf16[768,576]{0,1:T(8,128)(2,1)}, u32[]{:S(2)}, u32[]{:S(2)}) collective-permute-start(bf16[768,576]{0,1:T(8,128)(2,1)} %bitcast.406), channel_id=1, source_target_pairs={{0,1},{1,0},{2,3},{3,2},{4,5},{5,4},{6,7},{7,6},{8,9},{9,8},{10,11... | collective-permute-start | bytes 2654216 | tf_op jit(solution)/shard_map/ppermute | solution.py:120
  3.9 37.4 %collective-permute-start.3 = (bf16[384,576]{0,1:T(8,128)(2,1)}, bf16[384,576]{0,1:T(8,128)(2,1)}, u32[]{:S(2)}, u32[]{:S(2)}) collective-permute-start(bf16[384,576]{0,1:T(8,128)(2,1)} %constant_dynamic-slice_fusion.4), channel_id=1, source_target_pairs={{0,2},{1,3},{2,0},{3,1},{4,6},{5,7},{6,4},{7,5},{8,10},{9,11},{10,... | collective-permute-start | bytes 1327112 | tf_op jit(solution)/shard_map/ppermute | solution.py:120
  7.0 32.8 %collective-permute-start.6 = (bf16[96,768]{1,0:T(8,128)(2,1)}, bf16[96,768]{1,0:T(8,128)(2,1)}, u32[]{:S(2)}, u32[]{:S(2)}) collective-permute-start(bf16[96,768]{1,0:T(8,128)(2,1)} %constant_dynamic-slice_fusion.3), channel_id=1, source_target_pairs={{0,2},{1,3},{2,0},{3,1},{4,6},{5,7},{6,4},{7,5},{8,10},{9,11},{10,... | collective-permute-start | bytes 442376 | tf_op jit(solution)/shard_map/ppermute | solution.py:120
  9.5 38.3 %collective-permute-start.12 = (bf16[384,768]{1,0:T(8,128)(2,1)}, bf16[384,768]{1,0:T(8,128)(2,1)}, u32[]{:S(2)}, u32[]{:S(2)}) collective-permute-start(bf16[384,768]{1,0:T(8,128)(2,1)} %constant_dynamic-slice_fusion.2), channel_id=1, source_target_pairs={{0,2},{1,3},{2,0},{3,1},{4,6},{5,7},{6,4},{7,5},{8,10},{9,11},{10,... | collective-permute-start | bytes 1769480 | tf_op jit(solution)/shard_map/ppermute | solution.py:120
  13.8 18.4 %collective-permute-start.5 = (f32[2,1152]{1,0:T(2,128)S(1)}, f32[2,1152]{1,0:T(2,128)S(1)}, u32[]{:S(2)}, u32[]{:S(2)}) collective-permute-start(f32[2,1152]{1,0:T(2,128)S(1)} %pad_maximum_fusion.10), channel_id=1, source_target_pairs={{0,2},{1,3},{2,0},{3,1},{4,6},{5,7},{6,4},{7,5},{8,10},{9,11},{10,... | collective-permute-start | bytes 27656 | tf_op jit(solution)/shard_map/ppermute | solution.py:120
  46.7 32.4 %collective-permute-start.2 = (bf16[192,768]{1,0:T(8,128)(2,1)}, bf16[192,768]{1,0:T(8,128)(2,1)}, u32[]{:S(2)}, u32[]{:S(2)}) collective-permute-start(bf16[192,768]{1,0:T(8,128)(2,1)} %param.22), channel_id=1, source_target_pairs={{0,1},{1,0},{2,3},{3,2},{4,5},{5,4},{6,7},{7,6},{8,9},{9,8},{10,11... | collective-permute-start | bytes 884744 | tf_op jit(solution)/shard_map/ppermute | solution.py:120
  47.8 62.0 %collective-permute-start.10 = (bf16[768,768]{1,0:T(8,128)(2,1)}, bf16[768,768]{1,0:T(8,128)(2,1)}, u32[]{:S(2)}, u32[]{:S(2)}) collective-permute-start(bf16[768,768]{1,0:T(8,128)(2,1)} %param.26), channel_id=1, source_target_pairs={{0,1},{1,0},{2,3},{3,2},{4,5},{5,4},{6,7},{7,6},{8,9},{9,8},{10,11... | collective-permute-start | bytes 3538952 | tf_op jit(solution)/shard_map/ppermute | solution.py:120
  48.4 33.8 %collective-permute-start.13 = (bf16[384,768]{1,0:T(8,128)(2,1)}, bf16[384,768]{1,0:T(8,128)(2,1)}, u32[]{:S(2)}, u32[]{:S(2)}) collective-permute-start(bf16[384,768]{1,0:T(8,128)(2,1)} %collective-permute-done.12), channel_id=1, source_target_pairs={{0,4},{1,5},{2,6},{3,7},{4,0},{5,1},{6,2},{7,3},{8,12},{9,13},{10,... | collective-permute-start | bytes 1769480 | tf_op jit(solution)/shard_map/ppermute | solution.py:120
  56.2 28.9 %collective-permute-start.15 = (bf16[384,768]{1,0:T(8,128)(2,1)}, bf16[384,768]{1,0:T(8,128)(2,1)}, u32[]{:S(2)}, u32[]{:S(2)}) collective-permute-start(bf16[384,768]{1,0:T(8,128)(2,1)} %collective-permute-done.14), channel_id=1, source_target_pairs={{0,4},{1,5},{2,6},{3,7},{4,0},{5,1},{6,2},{7,3},{8,12},{9,13},{10,... | collective-permute-start | bytes 1769480 | tf_op jit(solution)/shard_map/ppermute | solution.py:120
  66.6 22.0 %collective-permute-start.8 = (bf16[768,576]{0,1:T(8,128)(2,1)}, bf16[768,576]{0,1:T(8,128)(2,1)}, u32[]{:S(2)}, u32[]{:S(2)}) collective-permute-start(bf16[768,576]{0,1:T(8,128)(2,1)} %copy-done.24), channel_id=1, source_target_pairs={{0,1},{1,0},{2,3},{3,2},{4,5},{5,4},{6,7},{7,6},{8,9},{9,8},{10,11... | collective-permute-start | bytes 2654216 | tf_op jit(solution)/shard_map/ppermute | solution.py:120
  79.1 36.1 %collective-permute-start.11 = (bf16[768,768]{1,0:T(8,128)(2,1)}, bf16[768,768]{1,0:T(8,128)(2,1)}, u32[]{:S(2)}, u32[]{:S(2)}) collective-permute-start(bf16[768,768]{1,0:T(8,128)(2,1)} %param.28), channel_id=1, source_target_pairs={{0,1},{1,0},{2,3},{3,2},{4,5},{5,4},{6,7},{7,6},{8,9},{9,8},{10,11... | collective-permute-start | bytes 3538952 | tf_op jit(solution)/shard_map/ppermute | solution.py:120
  85.1 38.0 %collective-permute-start.16 = (bf16[768,768]{1,0:T(8,128)(2,1)}, bf16[768,768]{1,0:T(8,128)(2,1)}, u32[]{:S(2)}, u32[]{:S(2)}) collective-permute-start(bf16[768,768]{1,0:T(8,128)(2,1)} %maximum_select_fusion), channel_id=1, source_target_pairs={{0,1},{1,0},{2,3},{3,2},{4,5},{5,4},{6,7},{7,6},{8,9},{9,8},{10,11... | collective-permute-start | bytes 3538952 | tf_op jit(solution)/shard_map/ppermute | solution.py:120
  88.6 40.4 %collective-permute-start.17 = (bf16[768,768]{1,0:T(8,128)(2,1)}, bf16[768,768]{1,0:T(8,128)(2,1)}, u32[]{:S(2)}, u32[]{:S(2)}) collective-permute-start(bf16[768,768]{1,0:T(8,128)(2,1)} %maximum_select_fusion.1), channel_id=1, source_target_pairs={{0,1},{1,0},{2,3},{3,2},{4,5},{5,4},{6,7},{7,6},{8,9},{9,8},{10,11... | collective-permute-start | bytes 3538952 | tf_op jit(solution)/shard_map/ppermute | solution.py:120
  213.8 29.7 %collective-permute-start.18 = (bf16[2,768,576]{1,2,0:T(8,128)(2,1)}, bf16[2,768,576]{1,2,0:T(8,128)(2,1)}, u32[]{:S(2)}, u32[]{:S(2)}) collective-permute-start(bf16[2,768,576]{1,2,0:T(8,128)(2,1)} %pad_maximum_fusion.2), channel_id=1, source_target_pairs={{0,1},{1,0},{2,3},{3,2},{4,5},{5,4},{6,7},{7,6},{8,9},{9,8},{10,11... | collective-permute-start | bytes 5308424 | tf_op jit(solution)/shard_map/ppermute | solution.py:120
  215.9 36.3 %collective-permute-start.31 = (bf16[2,192,768]{2,1,0:T(8,128)(2,1)S(1)}, bf16[2,192,768]{2,1,0:T(8,128)(2,1)S(1)}, u32[]{:S(2)}, u32[]{:S(2)}) collective-permute-start(bf16[2,192,768]{2,1,0:T(8,128)(2,1)S(1)} %pad_maximum_fusion.4), channel_id=1, source_target_pairs={{0,1},{1,0},{2,3},{3,2},{4,5},{5,4},{6,7},{7,6},{8,9},{9,8},{10,11... | collective-permute-start | bytes 1769480 | tf_op jit(solution)/shard_map/ppermute | solution.py:120
  218.4 27.9 %collective-permute-start.38 = (bf16[2,768,768]{2,1,0:T(8,128)(2,1)S(1)}, bf16[2,768,768]{2,1,0:T(8,128)(2,1)S(1)}, u32[]{:S(2)}, u32[]{:S(2)}) collective-permute-start(bf16[2,768,768]{2,1,0:T(8,128)(2,1)S(1)} %pad_maximum_fusion), channel_id=1, source_target_pairs={{0,1},{1,0},{2,3},{3,2},{4,5},{5,4},{6,7},{7,6},{8,9},{9,8},{10,11... | collective-permute-start | bytes 7077896 | tf_op jit(solution)/shard_map/ppermute | solution.py:120
  218.9 29.9 %collective-permute-start.45 = (bf16[2,768,768]{2,1,0:T(8,128)(2,1)S(1)}, bf16[2,768,768]{2,1,0:T(8,128)(2,1)S(1)}, u32[]{:S(2)}, u32[]{:S(2)}) collective-permute-start(bf16[2,768,768]{2,1,0:T(8,128)(2,1)S(1)} %pad_maximum_fusion.1), channel_id=1, source_target_pairs={{0,1},{1,0},{2,3},{3,2},{4,5},{5,4},{6,7},{7,6},{8,9},{9,8},{10,11... | collective-permute-start | bytes 7077896 | tf_op jit(solution)/shard_map/ppermute | solution.py:120
  245.7 75.6 %collective-permute-start.19 = (bf16[768,576]{0,1:T(8,128)(2,1)S(1)}, bf16[768,576]{0,1:T(8,128)(2,1)S(1)}, u32[]{:S(2)}, u32[]{:S(2)}) collective-permute-start(bf16[768,576]{0,1:T(8,128)(2,1)S(1)} %get-tuple-element.42), channel_id=1, source_target_pairs={{0,2},{1,3},{2,0},{3,1},{4,6},{5,7},{6,4},{7,5},{8,10},{9,11},{10,... | collective-permute-start | bytes 2654216 | tf_op jit(solution)/shard_map/ppermute | solution.py:120
  247.3 75.7 %collective-permute-start.39 = (bf16[768,768]{1,0:T(8,128)(2,1)S(1)}, bf16[768,768]{1,0:T(8,128)(2,1)S(1)}, u32[]{:S(2)}, u32[]{:S(2)}) collective-permute-start(bf16[768,768]{1,0:T(8,128)(2,1)S(1)} %get-tuple-element.40), channel_id=1, source_target_pairs={{0,2},{1,3},{2,0},{3,1},{4,6},{5,7},{6,4},{7,5},{8,10},{9,11},{10,... | collective-permute-start | bytes 3538952 | tf_op jit(solution)/shard_map/ppermute | solution.py:120
  249.8 73.9 %collective-permute-start.46 = (bf16[768,768]{1,0:T(8,128)(2,1)S(1)}, bf16[768,768]{1,0:T(8,128)(2,1)S(1)}, u32[]{:S(2)}, u32[]{:S(2)}) collective-permute-start(bf16[768,768]{1,0:T(8,128)(2,1)S(1)} %get-tuple-element.38), channel_id=1, source_target_pairs={{0,2},{1,3},{2,0},{3,1},{4,6},{5,7},{6,4},{7,5},{8,10},{9,11},{10,... | collective-permute-start | bytes 3538952 | tf_op jit(solution)/shard_map/ppermute | solution.py:120
  252.6 68.1 %collective-permute-start.32 = (bf16[192,768]{1,0:T(8,128)(2,1)S(1)}, bf16[192,768]{1,0:T(8,128)(2,1)S(1)}, u32[]{:S(2)}, u32[]{:S(2)}) collective-permute-start(bf16[192,768]{1,0:T(8,128)(2,1)S(1)} %get-tuple-element.45), channel_id=1, source_target_pairs={{0,2},{1,3},{2,0},{3,1},{4,6},{5,7},{6,4},{7,5},{8,10},{9,11},{10,... | collective-permute-start | bytes 884744 | tf_op jit(solution)/shard_map/ppermute | solution.py:120
  323.1 26.4 %collective-permute-start.40 = (bf16[384,768]{1,0:T(8,128)(2,1)S(1)}, bf16[384,768]{1,0:T(8,128)(2,1)S(1)}, u32[]{:S(2)}, u32[]{:S(2)}) collective-permute-start(bf16[384,768]{1,0:T(8,128)(2,1)S(1)} %add_convert_fusion.9), channel_id=1, source_target_pairs={{0,4},{1,5},{2,6},{3,7},{4,0},{5,1},{6,2},{7,3},{8,12},{9,13},{10,... | collective-permute-start | bytes 1769480 | tf_op jit(solution)/shard_map/ppermute | solution.py:120
  323.9 33.0 %collective-permute-start.47 = (bf16[384,768]{1,0:T(8,128)(2,1)S(1)}, bf16[384,768]{1,0:T(8,128)(2,1)S(1)}, u32[]{:S(2)}, u32[]{:S(2)}) collective-permute-start(bf16[384,768]{1,0:T(8,128)(2,1)S(1)} %add_convert_fusion.4), channel_id=1, source_target_pairs={{0,4},{1,5},{2,6},{3,7},{4,0},{5,1},{6,2},{7,3},{8,12},{9,13},{10,... | collective-permute-start | bytes 1769480 | tf_op jit(solution)/shard_map/ppermute | solution.py:120
  327.5 30.9 %collective-permute-start.34 = (bf16[96,768]{1,0:T(8,128)(2,1)S(1)}, bf16[96,768]{1,0:T(8,128)(2,1)S(1)}, u32[]{:S(2)}, u32[]{:S(2)}) collective-permute-start(bf16[96,768]{1,0:T(8,128)(2,1)S(1)} %add_convert_fusion.18), channel_id=1, source_target_pairs={{0,8},{1,9},{2,10},{3,11},{4,12},{5,13},{6,14},{7,15},{24,16},{25,... | collective-permute-start | bytes 442376 | tf_op jit(solution)/shard_map/ppermute | solution.py:120
  337.1 24.8 %collective-permute-start.21 = (bf16[384,576]{0,1:T(8,128)(2,1)S(1)}, bf16[384,576]{0,1:T(8,128)(2,1)S(1)}, u32[]{:S(2)}, u32[]{:S(2)}) collective-permute-start(bf16[384,576]{0,1:T(8,128)(2,1)S(1)} %add_convert_fusion.13), channel_id=1, source_target_pairs={{0,8},{1,9},{2,10},{3,11},{4,12},{5,13},{6,14},{7,15},{24,16},{25,... | collective-permute-start | bytes 1327112 | tf_op jit(solution)/shard_map/ppermute | solution.py:120
  358.5 19.4 %collective-permute-start.35 = (bf16[96,768]{1,0:T(8,128)(2,1)S(1)}, bf16[96,768]{1,0:T(8,128)(2,1)S(1)}, u32[]{:S(2)}, u32[]{:S(2)}) collective-permute-start(bf16[96,768]{1,0:T(8,128)(2,1)S(1)} %add_convert_fusion.17), channel_id=1, source_target_pairs={{8,16},{9,17},{10,18},{11,19},{12,20},{13,21},{14,22},{15,23},{16,... | collective-permute-start | bytes 442376 | tf_op jit(solution)/shard_map/ppermute | solution.py:120
  367.0 22.6 %collective-permute-start.42 = (bf16[384,768]{1,0:T(8,128)(2,1)S(1)}, bf16[384,768]{1,0:T(8,128)(2,1)S(1)}, u32[]{:S(2)}, u32[]{:S(2)}) collective-permute-start(bf16[384,768]{1,0:T(8,128)(2,1)S(1)} %add_convert_fusion.7), channel_id=1, source_target_pairs={{8,16},{9,17},{10,18},{11,19},{12,20},{13,21},{14,22},{15,23},{16,... | collective-permute-start | bytes 1769480 | tf_op jit(solution)/shard_map/ppermute | solution.py:120
  374.4 23.0 %collective-permute-start.49 = (bf16[384,768]{1,0:T(8,128)(2,1)S(1)}, bf16[384,768]{1,0:T(8,128)(2,1)S(1)}, u32[]{:S(2)}, u32[]{:S(2)}) collective-permute-start(bf16[384,768]{1,0:T(8,128)(2,1)S(1)} %add_convert_fusion.2), channel_id=1, source_target_pairs={{8,16},{9,17},{10,18},{11,19},{12,20},{13,21},{14,22},{15,23},{16,... | collective-permute-start | bytes 1769480 | tf_op jit(solution)/shard_map/ppermute | solution.py:120
  378.0 20.9 %collective-permute-start.36 = (bf16[96,768]{1,0:T(8,128)(2,1)S(1)}, bf16[96,768]{1,0:T(8,128)(2,1)S(1)}, u32[]{:S(2)}, u32[]{:S(2)}) collective-permute-start(bf16[96,768]{1,0:T(8,128)(2,1)S(1)} %add_convert_fusion.16), channel_id=1, source_target_pairs={{8,0},{9,1},{10,2},{11,3},{12,4},{13,5},{14,6},{15,7},{16,24},{17,... | collective-permute-start | bytes 442376 | tf_op jit(solution)/shard_map/ppermute | solution.py:120
  379.4 20.1 %collective-permute-start.23 = (bf16[384,576]{0,1:T(8,128)(2,1)S(1)}, bf16[384,576]{0,1:T(8,128)(2,1)S(1)}, u32[]{:S(2)}, u32[]{:S(2)}) collective-permute-start(bf16[384,576]{0,1:T(8,128)(2,1)S(1)} %add_convert_fusion.11), channel_id=1, source_target_pairs={{8,0},{9,1},{10,2},{11,3},{12,4},{13,5},{14,6},{15,7},{16,24},{17,... | collective-permute-start | bytes 1327112 | tf_op jit(solution)/shard_map/ppermute | solution.py:120
  404.6 23.3 %collective-permute-start.44 = (bf16[384,768]{1,0:T(8,128)(2,1)S(1)}, bf16[384,768]{1,0:T(8,128)(2,1)}, u32[]{:S(2)}, u32[]{:S(2)}) collective-permute-start(bf16[384,768]{1,0:T(8,128)(2,1)S(1)} %broadcast_select_fusion.1), channel_id=1, source_target_pairs={{0,4},{1,5},{2,6},{3,7},{4,0},{5,1},{6,2},{7,3},{8,12},{9,13},{10,... | collective-permute-start | bytes 1769480 | tf_op jit(solution)/shard_map/ppermute | solution.py:120
  412.2 22.5 %collective-permute-start.51 = (bf16[384,768]{1,0:T(8,128)(2,1)S(1)}, bf16[384,768]{1,0:T(8,128)(2,1)S(1)}, u32[]{:S(2)}, u32[]{:S(2)}) collective-permute-start(bf16[384,768]{1,0:T(8,128)(2,1)S(1)} %broadcast_select_fusion), channel_id=1, source_target_pairs={{0,4},{1,5},{2,6},{3,7},{4,0},{5,1},{6,2},{7,3},{8,12},{9,13},{10,... | collective-permute-start | bytes 1769480 | tf_op jit(solution)/shard_map/ppermute | solution.py:120
  (126 other events, 645.3 us)

commit v2 on v1

--- a/solution.py
+++ b/solution.py
@@ -268,13 +268,13 @@
     grad_two = norm_backward(grad_y, unit_two, inverse_two, gain_two)
     g_back_bias = jnp.sum(grad_two, axis=0)
     grad_ffn = grad_two.astype(BF16)
-    g_back = moves.reduce(
-        [
-            jnp.einsum("rf,rd->fd", activations[part], grad_ffn, preferred_element_type=F32)
-            for part in range(tp_count)
-        ]
-    )
+    back_terms = [
+        jnp.einsum("rf,rd->fd", activations[part], grad_ffn, preferred_element_type=F32)
+        for part in range(tp_count)
+    ]
     grad_preacts, g_in_bias = [], []
+    back_terms, grad_ffn = lax.optimization_barrier((back_terms, grad_ffn))
+    g_back = moves.reduce(back_terms)
     grad_normed = grad_two
     for part in range(tp_count):
         grad_act = jnp.einsum(
@@ -283,12 +283,12 @@
         grad_preact = (grad_act * gelu_slope(preacts[part])).astype(BF16)
         grad_preacts.append(grad_preact)
         g_in_bias.append(jnp.sum(grad_preact.astype(F32), axis=0))
-    g_in = moves.reduce(
-        [
-            jnp.einsum("rd,rf->df", normed_low, grad_preacts[part], preferred_element_type=F32)
-            for part in range(tp_count)
-        ]
-    )
+    in_terms = [
+        jnp.einsum("rd,rf->df", normed_low, grad_preacts[part], preferred_element_type=F32)
+        for part in range(tp_count)
+    ]
+    in_terms, grad_preacts = lax.optimization_barrier((in_terms, grad_preacts))
+    g_in = moves.reduce(in_terms)
     for part in range(tp_count):
         grad_normed = grad_normed + jnp.einsum(
             "rf,df->rd", grad_preacts[part], in_parts[part], preferred_element_type=F32
@@ -298,12 +298,12 @@
     grad_one = norm_backward(grad_normed, unit_one, inverse_one, gain_one)
     g_out_bias = jnp.sum(grad_one, axis=0)
     grad_attn = grad_one.astype(BF16)
-    g_out = moves.reduce(
-        [
-            jnp.einsum("rc,rd->cd", contexts[part], grad_attn, preferred_element_type=F32)
-            for part in range(tp_count)
-        ]
-    )
+    out_terms = [
+        jnp.einsum("rc,rd->cd", contexts[part], grad_attn, preferred_element_type=F32)
+        for part in range(tp_count)
+    ]
+    out_terms, grad_attn = lax.optimization_barrier((out_terms, grad_attn))
+    g_out = moves.reduce(out_terms)
     grad_flats, g_query, g_value = [], [], []
     grad_x = grad_one
     for part in range(tp_count):

time: 443 us -> 439 us (level)
  matrix products: 125 us -> 120 us
    unnamed x228 -> x182, local copies, waits for them, and re-layouts: 10.7 us -> 13.4 us
  transfers between devices with their start and end apart: 52 -> 52, of which waited for: 19 -> 20; matrix products, arithmetic and copies ran while one was open for 25% -> 25% of each run, Pallas kernels for 0% -> 0%
where the time goes in v2:
time: 439 us; the launch traced here: 432 us
  waiting for transfers between devices  176 us (40%)
  matrix products  120 us (27%)
  starting transfers between devices  57.7 us (13%)
  local copies, waits for them, and re-layouts  46.6 us (11%)
  other arithmetic  30.1 us (7%)
    ppermute x52, waiting for transfers between devices, send(): return lax.ppermute(value, AXES, pairs)  176 us
    ppermute x52, starting transfers between devices, send(): return lax.ppermute(value, AXES, pairs)  57.7 us
    dot_general x4, matrix products, body(): jnp.dot(normed_low, in_parts[part], preferred_element_type=F32)  22.5 us
    unnamed x182, local copies, waits for them, and re-layouts  13.4 us
    dot_general x4, matrix products, body(): jnp.einsum('rd,fd->rf', grad_ffn, back_parts[part], preferred_element_typ...  10.1 us
    dot_general x4, matrix products, body(): jnp.einsum('rf,df->rd', grad_preacts[part], in_parts[part], preferred_ele...  9.16 us
  transfers between devices with their start and end apart: 52, of which 20 were waited for; matrix products, arithmetic and copies ran while one was open for 25% of the time, Pallas kernels for 0%

profile of v2, /device:TPU:16, one launch (start us, length us, event | category | flops | bytes accessed | tf_op | source)
XLA Modules:
  0.0 432.2 jit_solution(196956657890009245)
XLA Ops:
  14.8 17.4 %collective-permute-done.5 = f32[2,1152]{1,0:T(2,128)S(1)} collective-permute-done((f32[2,1152]{1,0:T(2,128)S(1)}, f32[2,1152]{1,0:T(2,128)S(1)}, u32[]{:S(2)}, u32[]{:S(2)}) %collective-permute-start.5) | collective-permute-done | bytes 9248 | tf_op jit(solution)/shard_map/ppermute | solution.py:120
  41.5 4.9 %collective-permute-done.7 = bf16[96,768]{1,0:T(8,128)(2,1)S(1)} collective-permute-done((bf16[96,768]{1,0:T(8,128)(2,1)}, bf16[96,768]{1,0:T(8,128)(2,1)S(1)}, u32[]{:S(2)}, u32[]{:S(2)}) %collective-permute-start.7) | collective-permute-done | bytes 147488 | tf_op jit(solution)/shard_map/ppermute | solution.py:120
  49.5 6.3 %collective-permute-done.4 = bf16[384,576]{0,1:T(8,128)(2,1)S(1)} collective-permute-done((bf16[384,576]{0,1:T(8,128)(2,1)}, bf16[384,576]{0,1:T(8,128)(2,1)S(1)}, u32[]{:S(2)}, u32[]{:S(2)}) %collective-permute-start.4) | collective-permute-done | bytes 442400 | tf_op jit(solution)/shard_map/ppermute | solution.py:120
  61.2 2.9 reshape.377
  66.3 2.6 fusion.78
  68.9 2.6 reshape.375
  81.7 3.0 maximum_select_fusion
  85.2 2.9 maximum_select_fusion.1
  88.1 2.6 fusion.83
  90.8 2.6 reshape.379
  100.9 6.0 %fusion.8 = (bf16[512,768]{1,0:T(8,128)(2,1)S(1)}, f32[512,768]{1,0:T(8,128)S(1)}) fusion(f32[768]{0:T(1024)S(1)} %convert_element_type.552, bf16[512,768]{1,0:T(8,128)(2,1)S(1)} %fusion.76, bf16[768,768]{1,0:T(8,128)(2,1)} %param.26), kind=kOutput, calls=%fused_computation.25 | convolution fusion | flops 629932032 | bytes 4328448 | tf_op jit(solution)/shard_map/dot_general | solution.py:255
  108.9 5.5 %fusion.11 = (bf16[512,768]{1,0:T(8,128)(2,1)S(1)}, f32[512,768]{1,0:T(8,128)S(1)}) fusion(f32[768]{0:T(1024)S(1)} %copy-done.82, bf16[512,768]{1,0:T(8,128)(2,1)S(1)} %fusion.76, bf16[768,768]{1,0:T(8,128)(2,1)} %collective-permute-done.10), kind=kOutput, calls=%fused_computation.28 | convolution fusion | flops 629932032 | bytes 4328448 | tf_op jit(solution)/shard_map/dot_general | solution.py:255
  116.5 5.4 %fusion.14 = (bf16[512,768]{1,0:T(8,128)(2,1)S(1)}, f32[512,768]{1,0:T(8,128)S(1)}) fusion(f32[768]{0:T(1024)S(1)} %get-tuple-element.59, bf16[512,768]{1,0:T(8,128)(2,1)S(1)} %fusion.76, bf16[768,768]{1,0:T(8,128)(2,1)} %maximum_select_fusion), kind=kOutput, calls=%fused_computation.31 | convolution fusion | flops 629932032 | bytes 4328448 | tf_op jit(solution)/shard_map/dot_general | solution.py:255
  122.0 5.6 %fusion.17 = (bf16[512,768]{1,0:T(8,128)(2,1)S(1)}, f32[512,768]{1,0:T(8,128)S(1)}) fusion(f32[768]{0:T(1024)S(1)} %get-tuple-element.60, bf16[512,768]{1,0:T(8,128)(2,1)S(1)} %fusion.76, bf16[768,768]{1,0:T(8,128)(2,1)} %collective-permute-done.16), kind=kOutput, calls=%fused_computation.34 | convolution fusion | flops 629932032 | bytes 4328448 | tf_op jit(solution)/shard_map/dot_general | solution.py:255
  145.6 3.0 convert_reduce_fusion.3
  168.1 2.9 multiply_reduce_fusion.1
  219.6 4.5 %collective-permute-done.25 = f32[9216]{0:T(1024)S(1)} collective-permute-done((f32[9216]{0:T(1024)S(1)}, f32[9216]{0:T(1024)S(1)}, u32[]{:S(2)}, u32[]{:S(2)}) %collective-permute-start.25) | collective-permute-done | bytes 36896 | tf_op jit(solution)/shard_map/ppermute | solution.py:120
  237.9 2.6 collective-permute-start.29
  251.8 64.2 %collective-permute-done.32 = bf16[192,768]{1,0:T(8,128)(2,1)S(1)} collective-permute-done((bf16[192,768]{1,0:T(8,128)(2,1)S(1)}, bf16[192,768]{1,0:T(8,128)(2,1)S(1)}, u32[]{:S(2)}, u32[]{:S(2)}) %collective-permute-start.32) | collective-permute-done | bytes 294944 | tf_op jit(solution)/shard_map/ppermute | solution.py:120
  324.2 8.1 %collective-permute-done.20 = bf16[384,576]{0,1:T(8,128)(2,1)S(1)} collective-permute-done((bf16[384,576]{0,1:T(8,128)(2,1)S(1)}, bf16[384,576]{0,1:T(8,128)(2,1)S(1)}, u32[]{:S(2)}, u32[]{:S(2)}) %collective-permute-start.20) | collective-permute-done | bytes 442400 | tf_op jit(solution)/shard_map/ppermute | solution.py:120
  333.8 11.2 %collective-permute-done.40 = bf16[384,768]{1,0:T(8,128)(2,1)S(1)} collective-permute-done((bf16[384,768]{1,0:T(8,128)(2,1)S(1)}, bf16[384,768]{1,0:T(8,128)(2,1)S(1)}, u32[]{:S(2)}, u32[]{:S(2)}) %collective-permute-start.40) | collective-permute-done | bytes 589856 | tf_op jit(solution)/shard_map/ppermute | solution.py:120
  346.5 5.7 %collective-permute-done.47 = bf16[384,768]{1,0:T(8,128)(2,1)S(1)} collective-permute-done((bf16[384,768]{1,0:T(8,128)(2,1)S(1)}, bf16[384,768]{1,0:T(8,128)(2,1)S(1)}, u32[]{:S(2)}, u32[]{:S(2)}) %collective-permute-start.47) | collective-permute-done | bytes 589856 | tf_op jit(solution)/shard_map/ppermute | solution.py:120
  353.8 3.5 collective-permute-start.35
  362.5 3.5 collective-permute-start.42
  366.0 3.6 collective-permute-done.48
  369.8 3.5 collective-permute-start.49
  376.1 8.9 %collective-permute-done.42 = bf16[384,768]{1,0:T(8,128)(2,1)S(1)} collective-permute-done((bf16[384,768]{1,0:T(8,128)(2,1)S(1)}, bf16[384,768]{1,0:T(8,128)(2,1)S(1)}, u32[]{:S(2)}, u32[]{:S(2)}) %collective-permute-start.42) | collective-permute-done | bytes 589856 | tf_op jit(solution)/shard_map/ppermute | solution.py:120
  386.5 6.2 %collective-permute-done.49 = bf16[384,768]{1,0:T(8,128)(2,1)S(1)} collective-permute-done((bf16[384,768]{1,0:T(8,128)(2,1)S(1)}, bf16[384,768]{1,0:T(8,128)(2,1)S(1)}, u32[]{:S(2)}, u32[]{:S(2)}) %collective-permute-start.49) | collective-permute-done | bytes 589856 | tf_op jit(solution)/shard_map/ppermute | solution.py:120
  396.4 3.5 collective-permute-done.43
  401.4 6.0 %collective-permute-done.50 = bf16[384,768]{1,0:T(8,128)(2,1)S(1)} collective-permute-done((bf16[384,768]{1,0:T(8,128)(2,1)S(1)}, bf16[384,768]{1,0:T(8,128)(2,1)S(1)}, u32[]{:S(2)}, u32[]{:S(2)}) %collective-permute-start.50) | collective-permute-done | bytes 589856 | tf_op jit(solution)/shard_map/ppermute | solution.py:120
  414.7 8.4 %collective-permute-done.44 = bf16[384,768]{1,0:T(8,128)(2,1)S(1)} collective-permute-done((bf16[384,768]{1,0:T(8,128)(2,1)S(1)}, bf16[384,768]{1,0:T(8,128)(2,1)S(1)}, u32[]{:S(2)}, u32[]{:S(2)}) %collective-permute-start.44) | collective-permute-done | bytes 589856 | tf_op jit(solution)/shard_map/ppermute | solution.py:120
  424.7 5.7 %collective-permute-done.51 = bf16[384,768]{1,0:T(8,128)(2,1)S(1)} collective-permute-done((bf16[384,768]{1,0:T(8,128)(2,1)S(1)}, bf16[384,768]{1,0:T(8,128)(2,1)S(1)}, u32[]{:S(2)}, u32[]{:S(2)}) %collective-permute-start.51) | collective-permute-done | bytes 589856 | tf_op jit(solution)/shard_map/ppermute | solution.py:120
  (468 shorter events, 204.5 us)
Async XLA Ops:
  3.2 36.3 %collective-permute-start.6 = (bf16[96,768]{1,0:T(8,128)(2,1)}, bf16[96,768]{1,0:T(8,128)(2,1)}, u32[]{:S(2)}, u32[]{:S(2)}) collective-permute-start(bf16[96,768]{1,0:T(8,128)(2,1)} %constant_dynamic-slice_fusion.3), channel_id=1, source_target_pairs={{0,2},{1,3},{2,0},{3,1},{4,6},{5,7},{6,4},{7,5},{8,10},{9,11},{10,... | collective-permute-start | bytes 442376 | tf_op jit(solution)/shard_map/ppermute | solution.py:120
  4.7 61.6 %collective-permute-start = (bf16[768,576]{0,1:T(8,128)(2,1)}, bf16[768,576]{0,1:T(8,128)(2,1)}, u32[]{:S(2)}, u32[]{:S(2)}) collective-permute-start(bf16[768,576]{0,1:T(8,128)(2,1)} %bitcast.412), channel_id=1, source_target_pairs={{0,1},{1,0},{2,3},{3,2},{4,5},{5,4},{6,7},{7,6},{8,9},{9,8},{10,11... | collective-permute-start | bytes 2654216 | tf_op jit(solution)/shard_map/ppermute | solution.py:120
  6.7 34.3 %collective-permute-start.3 = (bf16[384,576]{0,1:T(8,128)(2,1)}, bf16[384,576]{0,1:T(8,128)(2,1)}, u32[]{:S(2)}, u32[]{:S(2)}) collective-permute-start(bf16[384,576]{0,1:T(8,128)(2,1)} %constant_dynamic-slice_fusion.4), channel_id=1, source_target_pairs={{0,2},{1,3},{2,0},{3,1},{4,6},{5,7},{6,4},{7,5},{8,10},{9,11},{10,... | collective-permute-start | bytes 1327112 | tf_op jit(solution)/shard_map/ppermute | solution.py:120
  9.2 38.2 %collective-permute-start.14 = (bf16[384,768]{1,0:T(8,128)(2,1)}, bf16[384,768]{1,0:T(8,128)(2,1)}, u32[]{:S(2)}, u32[]{:S(2)}) collective-permute-start(bf16[384,768]{1,0:T(8,128)(2,1)} %constant_dynamic-slice_fusion.1), channel_id=1, source_target_pairs={{0,2},{1,3},{2,0},{3,1},{4,6},{5,7},{6,4},{7,5},{8,10},{9,11},{10,... | collective-permute-start | bytes 1769480 | tf_op jit(solution)/shard_map/ppermute | solution.py:120
  13.5 18.7 %collective-permute-start.5 = (f32[2,1152]{1,0:T(2,128)S(1)}, f32[2,1152]{1,0:T(2,128)S(1)}, u32[]{:S(2)}, u32[]{:S(2)}) collective-permute-start(f32[2,1152]{1,0:T(2,128)S(1)} %pad_maximum_fusion.10), channel_id=1, source_target_pairs={{0,2},{1,3},{2,0},{3,1},{4,6},{5,7},{6,4},{7,5},{8,10},{9,11},{10,... | collective-permute-start | bytes 27656 | tf_op jit(solution)/shard_map/ppermute | solution.py:120
  46.4 32.2 %collective-permute-start.2 = (bf16[192,768]{1,0:T(8,128)(2,1)}, bf16[192,768]{1,0:T(8,128)(2,1)}, u32[]{:S(2)}, u32[]{:S(2)}) collective-permute-start(bf16[192,768]{1,0:T(8,128)(2,1)} %param.22), channel_id=1, source_target_pairs={{0,1},{1,0},{2,3},{3,2},{4,5},{5,4},{6,7},{7,6},{8,9},{9,8},{10,11... | collective-permute-start | bytes 884744 | tf_op jit(solution)/shard_map/ppermute | solution.py:120
  47.4 61.5 %collective-permute-start.10 = (bf16[768,768]{1,0:T(8,128)(2,1)}, bf16[768,768]{1,0:T(8,128)(2,1)}, u32[]{:S(2)}, u32[]{:S(2)}) collective-permute-start(bf16[768,768]{1,0:T(8,128)(2,1)} %param.26), channel_id=1, source_target_pairs={{0,1},{1,0},{2,3},{3,2},{4,5},{5,4},{6,7},{7,6},{8,9},{9,8},{10,11... | collective-permute-start | bytes 3538952 | tf_op jit(solution)/shard_map/ppermute | solution.py:120
  48.0 36.7 %collective-permute-start.15 = (bf16[384,768]{1,0:T(8,128)(2,1)}, bf16[384,768]{1,0:T(8,128)(2,1)}, u32[]{:S(2)}, u32[]{:S(2)}) collective-permute-start(bf16[384,768]{1,0:T(8,128)(2,1)} %collective-permute-done.14), channel_id=1, source_target_pairs={{0,4},{1,5},{2,6},{3,7},{4,0},{5,1},{6,2},{7,3},{8,12},{9,13},{10,... | collective-permute-start | bytes 1769480 | tf_op jit(solution)/shard_map/ppermute | solution.py:120
  55.9 25.9 %collective-permute-start.13 = (bf16[384,768]{1,0:T(8,128)(2,1)}, bf16[384,768]{1,0:T(8,128)(2,1)}, u32[]{:S(2)}, u32[]{:S(2)}) collective-permute-start(bf16[384,768]{1,0:T(8,128)(2,1)} %collective-permute-done.12), channel_id=1, source_target_pairs={{0,4},{1,5},{2,6},{3,7},{4,0},{5,1},{6,2},{7,3},{8,12},{9,13},{10,... | collective-permute-start | bytes 1769480 | tf_op jit(solution)/shard_map/ppermute | solution.py:120
  66.3 21.8 %collective-permute-start.8 = (bf16[768,576]{0,1:T(8,128)(2,1)}, bf16[768,576]{0,1:T(8,128)(2,1)}, u32[]{:S(2)}, u32[]{:S(2)}) collective-permute-start(bf16[768,576]{0,1:T(8,128)(2,1)} %copy-done.20), channel_id=1, source_target_pairs={{0,1},{1,0},{2,3},{3,2},{4,5},{5,4},{6,7},{7,6},{8,9},{9,8},{10,11... | collective-permute-start | bytes 2654216 | tf_op jit(solution)/shard_map/ppermute | solution.py:120
  78.6 35.8 %collective-permute-start.11 = (bf16[768,768]{1,0:T(8,128)(2,1)}, bf16[768,768]{1,0:T(8,128)(2,1)}, u32[]{:S(2)}, u32[]{:S(2)}) collective-permute-start(bf16[768,768]{1,0:T(8,128)(2,1)} %param.28), channel_id=1, source_target_pairs={{0,1},{1,0},{2,3},{3,2},{4,5},{5,4},{6,7},{7,6},{8,9},{9,8},{10,11... | collective-permute-start | bytes 3538952 | tf_op jit(solution)/shard_map/ppermute | solution.py:120
  84.8 37.2 %collective-permute-start.16 = (bf16[768,768]{1,0:T(8,128)(2,1)}, bf16[768,768]{1,0:T(8,128)(2,1)}, u32[]{:S(2)}, u32[]{:S(2)}) collective-permute-start(bf16[768,768]{1,0:T(8,128)(2,1)} %maximum_select_fusion), channel_id=1, source_target_pairs={{0,1},{1,0},{2,3},{3,2},{4,5},{5,4},{6,7},{7,6},{8,9},{9,8},{10,11... | collective-permute-start | bytes 3538952 | tf_op jit(solution)/shard_map/ppermute | solution.py:120
  88.1 39.5 %collective-permute-start.17 = (bf16[768,768]{1,0:T(8,128)(2,1)}, bf16[768,768]{1,0:T(8,128)(2,1)}, u32[]{:S(2)}, u32[]{:S(2)}) collective-permute-start(bf16[768,768]{1,0:T(8,128)(2,1)} %maximum_select_fusion.1), channel_id=1, source_target_pairs={{0,1},{1,0},{2,3},{3,2},{4,5},{5,4},{6,7},{7,6},{8,9},{9,8},{10,11... | collective-permute-start | bytes 3538952 | tf_op jit(solution)/shard_map/ppermute | solution.py:120
  204.6 45.2 %collective-permute-start.31 = (bf16[2,192,768]{2,1,0:T(8,128)(2,1)}, bf16[2,192,768]{2,1,0:T(8,128)(2,1)}, u32[]{:S(2)}, u32[]{:S(2)}) collective-permute-start(bf16[2,192,768]{2,1,0:T(8,128)(2,1)} %pad_maximum_fusion.4), channel_id=1, source_target_pairs={{0,1},{1,0},{2,3},{3,2},{4,5},{5,4},{6,7},{7,6},{8,9},{9,8},{10,11... | collective-permute-start | bytes 1769480 | tf_op jit(solution)/shard_map/ppermute | solution.py:120
  213.5 27.0 %collective-permute-start.18 = (bf16[2,768,576]{1,2,0:T(8,128)(2,1)S(1)}, bf16[2,768,576]{1,2,0:T(8,128)(2,1)S(1)}, u32[]{:S(2)}, u32[]{:S(2)}) collective-permute-start(bf16[2,768,576]{1,2,0:T(8,128)(2,1)S(1)} %pad_maximum_fusion.2), channel_id=1, source_target_pairs={{0,1},{1,0},{2,3},{3,2},{4,5},{5,4},{6,7},{7,6},{8,9},{9,8},{10,11... | collective-permute-start | bytes 5308424 | tf_op jit(solution)/shard_map/ppermute | solution.py:120
  215.2 26.8 %collective-permute-start.38 = (bf16[2,768,768]{2,1,0:T(8,128)(2,1)S(1)}, bf16[2,768,768]{2,1,0:T(8,128)(2,1)S(1)}, u32[]{:S(2)}, u32[]{:S(2)}) collective-permute-start(bf16[2,768,768]{2,1,0:T(8,128)(2,1)S(1)} %pad_maximum_fusion), channel_id=1, source_target_pairs={{0,1},{1,0},{2,3},{3,2},{4,5},{5,4},{6,7},{7,6},{8,9},{9,8},{10,11... | collective-permute-start | bytes 7077896 | tf_op jit(solution)/shard_map/ppermute | solution.py:120
  216.8 27.1 %collective-permute-start.45 = (bf16[2,768,768]{2,1,0:T(8,128)(2,1)S(1)}, bf16[2,768,768]{2,1,0:T(8,128)(2,1)S(1)}, u32[]{:S(2)}, u32[]{:S(2)}) collective-permute-start(bf16[2,768,768]{2,1,0:T(8,128)(2,1)S(1)} %pad_maximum_fusion.1), channel_id=1, source_target_pairs={{0,1},{1,0},{2,3},{3,2},{4,5},{5,4},{6,7},{7,6},{8,9},{9,8},{10,11... | collective-permute-start | bytes 7077896 | tf_op jit(solution)/shard_map/ppermute | solution.py:120
  241.1 76.0 %collective-permute-start.19 = (bf16[768,576]{0,1:T(8,128)(2,1)S(1)}, bf16[768,576]{0,1:T(8,128)(2,1)S(1)}, u32[]{:S(2)}, u32[]{:S(2)}) collective-permute-start(bf16[768,576]{0,1:T(8,128)(2,1)S(1)} %get-tuple-element.78), channel_id=1, source_target_pairs={{0,2},{1,3},{2,0},{3,1},{4,6},{5,7},{6,4},{7,5},{8,10},{9,11},{10,... | collective-permute-start | bytes 2654216 | tf_op jit(solution)/shard_map/ppermute | solution.py:120
  242.6 75.8 %collective-permute-start.39 = (bf16[768,768]{1,0:T(8,128)(2,1)S(1)}, bf16[768,768]{1,0:T(8,128)(2,1)S(1)}, u32[]{:S(2)}, u32[]{:S(2)}) collective-permute-start(bf16[768,768]{1,0:T(8,128)(2,1)S(1)} %get-tuple-element.76), channel_id=1, source_target_pairs={{0,2},{1,3},{2,0},{3,1},{4,6},{5,7},{6,4},{7,5},{8,10},{9,11},{10,... | collective-permute-start | bytes 3538952 | tf_op jit(solution)/shard_map/ppermute | solution.py:120
  244.9 74.6 %collective-permute-start.46 = (bf16[768,768]{1,0:T(8,128)(2,1)S(1)}, bf16[768,768]{1,0:T(8,128)(2,1)S(1)}, u32[]{:S(2)}, u32[]{:S(2)}) collective-permute-start(bf16[768,768]{1,0:T(8,128)(2,1)S(1)} %get-tuple-element.74), channel_id=1, source_target_pairs={{0,2},{1,3},{2,0},{3,1},{4,6},{5,7},{6,4},{7,5},{8,10},{9,11},{10,... | collective-permute-start | bytes 3538952 | tf_op jit(solution)/shard_map/ppermute | solution.py:120
  251.0 65.1 %collective-permute-start.32 = (bf16[192,768]{1,0:T(8,128)(2,1)S(1)}, bf16[192,768]{1,0:T(8,128)(2,1)S(1)}, u32[]{:S(2)}, u32[]{:S(2)}) collective-permute-start(bf16[192,768]{1,0:T(8,128)(2,1)S(1)} %get-tuple-element.81), channel_id=1, source_target_pairs={{0,2},{1,3},{2,0},{3,1},{4,6},{5,7},{6,4},{7,5},{8,10},{9,11},{10,... | collective-permute-start | bytes 884744 | tf_op jit(solution)/shard_map/ppermute | solution.py:120
  318.5 26.5 %collective-permute-start.40 = (bf16[384,768]{1,0:T(8,128)(2,1)S(1)}, bf16[384,768]{1,0:T(8,128)(2,1)S(1)}, u32[]{:S(2)}, u32[]{:S(2)}) collective-permute-start(bf16[384,768]{1,0:T(8,128)(2,1)S(1)} %add_convert_fusion.9), channel_id=1, source_target_pairs={{0,4},{1,5},{2,6},{3,7},{4,0},{5,1},{6,2},{7,3},{8,12},{9,13},{10,... | collective-permute-start | bytes 1769480 | tf_op jit(solution)/shard_map/ppermute | solution.py:120
  319.7 32.5 %collective-permute-start.47 = (bf16[384,768]{1,0:T(8,128)(2,1)S(1)}, bf16[384,768]{1,0:T(8,128)(2,1)S(1)}, u32[]{:S(2)}, u32[]{:S(2)}) collective-permute-start(bf16[384,768]{1,0:T(8,128)(2,1)S(1)} %add_convert_fusion.4), channel_id=1, source_target_pairs={{0,4},{1,5},{2,6},{3,7},{4,0},{5,1},{6,2},{7,3},{8,12},{9,13},{10,... | collective-permute-start | bytes 1769480 | tf_op jit(solution)/shard_map/ppermute | solution.py:120
  322.9 30.8 %collective-permute-start.34 = (bf16[96,768]{1,0:T(8,128)(2,1)S(1)}, bf16[96,768]{1,0:T(8,128)(2,1)S(1)}, u32[]{:S(2)}, u32[]{:S(2)}) collective-permute-start(bf16[96,768]{1,0:T(8,128)(2,1)S(1)} %add_convert_fusion.18), channel_id=1, source_target_pairs={{0,8},{1,9},{2,10},{3,11},{4,12},{5,13},{6,14},{7,15},{24,16},{25,... | collective-permute-start | bytes 442376 | tf_op jit(solution)/shard_map/ppermute | solution.py:120
  332.5 24.8 %collective-permute-start.21 = (bf16[384,576]{0,1:T(8,128)(2,1)S(1)}, bf16[384,576]{0,1:T(8,128)(2,1)S(1)}, u32[]{:S(2)}, u32[]{:S(2)}) collective-permute-start(bf16[384,576]{0,1:T(8,128)(2,1)S(1)} %add_convert_fusion.13), channel_id=1, source_target_pairs={{0,8},{1,9},{2,10},{3,11},{4,12},{5,13},{6,14},{7,15},{24,16},{25,... | collective-permute-start | bytes 1327112 | tf_op jit(solution)/shard_map/ppermute | solution.py:120
  353.8 19.5 %collective-permute-start.35 = (bf16[96,768]{1,0:T(8,128)(2,1)S(1)}, bf16[96,768]{1,0:T(8,128)(2,1)S(1)}, u32[]{:S(2)}, u32[]{:S(2)}) collective-permute-start(bf16[96,768]{1,0:T(8,128)(2,1)S(1)} %add_convert_fusion.17), channel_id=1, source_target_pairs={{8,16},{9,17},{10,18},{11,19},{12,20},{13,21},{14,22},{15,23},{16,... | collective-permute-start | bytes 442376 | tf_op jit(solution)/shard_map/ppermute | solution.py:120
  362.5 22.5 %collective-permute-start.42 = (bf16[384,768]{1,0:T(8,128)(2,1)S(1)}, bf16[384,768]{1,0:T(8,128)(2,1)S(1)}, u32[]{:S(2)}, u32[]{:S(2)}) collective-permute-start(bf16[384,768]{1,0:T(8,128)(2,1)S(1)} %add_convert_fusion.7), channel_id=1, source_target_pairs={{8,16},{9,17},{10,18},{11,19},{12,20},{13,21},{14,22},{15,23},{16,... | collective-permute-start | bytes 1769480 | tf_op jit(solution)/shard_map/ppermute | solution.py:120
  369.8 22.9 %collective-permute-start.49 = (bf16[384,768]{1,0:T(8,128)(2,1)S(1)}, bf16[384,768]{1,0:T(8,128)(2,1)S(1)}, u32[]{:S(2)}, u32[]{:S(2)}) collective-permute-start(bf16[384,768]{1,0:T(8,128)(2,1)S(1)} %add_convert_fusion.2), channel_id=1, source_target_pairs={{8,16},{9,17},{10,18},{11,19},{12,20},{13,21},{14,22},{15,23},{16,... | collective-permute-start | bytes 1769480 | tf_op jit(solution)/shard_map/ppermute | solution.py:120
  373.3 20.8 %collective-permute-start.36 = (bf16[96,768]{1,0:T(8,128)(2,1)S(1)}, bf16[96,768]{1,0:T(8,128)(2,1)S(1)}, u32[]{:S(2)}, u32[]{:S(2)}) collective-permute-start(bf16[96,768]{1,0:T(8,128)(2,1)S(1)} %add_convert_fusion.16), channel_id=1, source_target_pairs={{8,0},{9,1},{10,2},{11,3},{12,4},{13,5},{14,6},{15,7},{16,24},{17,... | collective-permute-start | bytes 442376 | tf_op jit(solution)/shard_map/ppermute | solution.py:120
  374.8 21.3 %collective-permute-start.23 = (bf16[384,576]{0,1:T(8,128)(2,1)S(1)}, bf16[384,576]{0,1:T(8,128)(2,1)S(1)}, u32[]{:S(2)}, u32[]{:S(2)}) collective-permute-start(bf16[384,576]{0,1:T(8,128)(2,1)S(1)} %add_convert_fusion.11), channel_id=1, source_target_pairs={{8,0},{9,1},{10,2},{11,3},{12,4},{13,5},{14,6},{15,7},{16,24},{17,... | collective-permute-start | bytes 1327112 | tf_op jit(solution)/shard_map/ppermute | solution.py:120
  399.9 23.1 %collective-permute-start.44 = (bf16[384,768]{1,0:T(8,128)(2,1)S(1)}, bf16[384,768]{1,0:T(8,128)(2,1)S(1)}, u32[]{:S(2)}, u32[]{:S(2)}) collective-permute-start(bf16[384,768]{1,0:T(8,128)(2,1)S(1)} %broadcast_select_fusion.1), channel_id=1, source_target_pairs={{0,4},{1,5},{2,6},{3,7},{4,0},{5,1},{6,2},{7,3},{8,12},{9,13},{10,... | collective-permute-start | bytes 1769480 | tf_op jit(solution)/shard_map/ppermute | solution.py:120
  407.5 23.0 %collective-permute-start.51 = (bf16[384,768]{1,0:T(8,128)(2,1)S(1)}, bf16[384,768]{1,0:T(8,128)(2,1)S(1)}, u32[]{:S(2)}, u32[]{:S(2)}) collective-permute-start(bf16[384,768]{1,0:T(8,128)(2,1)S(1)} %broadcast_select_fusion), channel_id=1, source_target_pairs={{0,4},{1,5},{2,6},{3,7},{4,0},{5,1},{6,2},{7,3},{8,12},{9,13},{10,... | collective-permute-start | bytes 1769480 | tf_op jit(solution)/shard_map/ppermute | solution.py:120
  (103 other events, 571.6 us)
